TPU v7x, 512 devices: a whole 4x4x16 slice. The times are simulated.
512 devices in a mesh: lat: 8 (over z_lo), lon: 16 (over x, z_hi, core), mp: 4 (over y).
Axes of the slice: x: 4, y: 4, z: 16 (z_hi: 2, z_lo: 8; z = z_hi * 8 + z_lo), core: 2. Of those that a mesh axis runs over, the one named last changes fastest.
Arguments:
- sharp_resolution_vectors: bfloat16 [2, 128, 256, 512], P(None, 'lat', 'lon'), may hold values from -6 to 6
- queries_keys_weights: bfloat16 [512, 2, 512], P(None, None, 'mp'), may hold values from -0.03125 to 0.03125
- values_weights: bfloat16 [512, 512], P(None, 'mp'), may hold values from -0.25 to 0.25
- attn_result_weights: bfloat16 [512, 512], P('mp'), may hold values from -0.75 to 0.75
- score_factors_by_lane: float32 [8], replicated, may hold values from 1 to 8
- tile_merging_weights: bfloat16 [2048, 1024], P('lon', 'mp'), may hold values from -0.125 to 0.125
- shrunk_dense_first: bfloat16 [1024, 4096], P('lon', 'mp'), may hold values from -0.1875 to 0.1875
- shrunk_dense_second: bfloat16 [4096, 1024], P('mp', 'lon'), may hold values from -0.09375 to 0.09375
- tile_unfolding_weights: bfloat16 [1024, 2048], P('lon', 'mp'), may hold values from -0.1875 to 0.1875
- result_gradient: bfloat16 [2, 128, 256, 512], P(None, 'lat', ('lon', 'mp')), may hold values from -6 to 6
Outputs:
- output: bfloat16 [2, 128, 256, 512], P(None, 'lat', ('lon', 'mp'))
- fine_grad: bfloat16 [2, 128, 256, 512], P(None, 'lat', ('lon', 'mp'))
All inputs are finite; a program needn't handle non-finite values.
Results may differ from a plain program's by a relative error of at most 0.02.
Values may be sent and summed in bfloat16 or wider, within the bound.
No kernel may reach another device: no remote copies, remote signals or barrier semaphores. Data moves between devices by JAX's collectives and lax.ppermute only.
A program may use at most 128 MiB of HBM per device.

v0:
```python
import jax
import jax.numpy as jnp
import numpy as np
from jax import lax
from jax.experimental import pallas as pl
from jax.experimental.pallas import tpu as pltpu
from jax.sharding import Mesh, PartitionSpec as P

BF, F32 = jnp.bfloat16, jnp.float32
EPS = 1e-05
LON = ("x", "zh", "core")
LONMP = LON + ("mp",)
ALL = ("lat",) + LONMP
STEPS = (0, 1, 3, 2)


def dot(a, b, ca=1, cb=0):
    return lax.dot_general(a, b, (((ca,), (cb,)), ((), ())), preferred_element_type=F32)


def to_all(value, axis):
    n = lax.axis_size(axis)
    return lax.all_to_all(
        jnp.broadcast_to(value[None], (n, *value.shape)), axis, 0, 0, tiled=True
    )


def swap(value, axis):
    return lax.all_to_all(value, axis, 0, 0, tiled=True)


def call(body, outs, scratch=(), n_scalar=0, n_in=0):
    specs = [pl.BlockSpec(memory_space=pltpu.SMEM)] * n_scalar + [
        pl.BlockSpec(memory_space=pltpu.VMEM)
    ] * n_in
    many = isinstance(outs, (list, tuple))
    ospecs = [pl.BlockSpec(memory_space=pltpu.VMEM)] * (len(outs) if many else 1)
    return pl.pallas_call(
        body,
        out_shape=outs,
        in_specs=specs,
        out_specs=ospecs if many else ospecs[0],
        scratch_shapes=list(scratch),
        compiler_params=pltpu.CompilerParams(vmem_limit_bytes=24 << 20),
    )


def arr(*shape, dtype=BF):
    return jax.ShapeDtypeStruct(shape, dtype)


def norm_parts(values, width):
    total = sum(jnp.sum(v, -1, keepdims=True) for v in values)
    mean = total / width
    centers = [v - mean for v in values]
    spread = sum(jnp.sum(c * c, -1, keepdims=True) for c in centers) / width
    return centers, lax.rsqrt(spread + EPS)


def norm_back(grads, centers, scale, width):
    normal = [c * scale for c in centers]
    mean_g = sum(jnp.sum(g, -1, keepdims=True) for g in grads) / width
    mean_gn = sum(jnp.sum(g * n, -1, keepdims=True) for g, n in zip(grads, normal)) / width
    return [scale * (g - mean_g - n * mean_gn) for g, n in zip(grads, normal)]


def segments():
    a = lax.broadcasted_iota(jnp.int32, (128, 128), 0) // 64
    b = lax.broadcasted_iota(jnp.int32, (128, 128), 1) // 64
    return jnp.where(a == b, 1.0, 0.0).astype(BF)


def head_sums(values, ones):
    high = values.astype(BF)
    low = (values - high.astype(F32)).astype(BF)
    return dot(high, ones) + dot(low, ones)


def by_head(v):
    lane = lax.broadcasted_iota(jnp.int32, v.shape, 1)
    zero = jnp.zeros_like(v)
    return jnp.concatenate([jnp.where(lane < 64, v, zero), jnp.where(lane < 64, zero, v)], 0)


def attend(q, k, scale_a, scale_b, split, ones):
    qf, kf = q.astype(F32), k.astype(F32)
    q_sum, k_sum = head_sums(qf * qf, ones), head_sums(kf * kf, ones)
    q_len = jnp.maximum(jnp.sqrt(q_sum), 1.0)
    k_len = jnp.maximum(jnp.sqrt(k_sum), 1.0)
    q_unit = (qf / q_len).astype(BF)
    k_unit = (kf / k_len).astype(BF)
    q_two = by_head(q_unit)
    row = lax.broadcasted_iota(jnp.int32, (256, 128), 0)
    col = lax.broadcasted_iota(jnp.int32, (256, 128), 1)
    scale = jnp.where(row < 128, scale_a, scale_b)
    raw = jnp.exp(dot(q_two, k_unit, 1, 1) * scale)
    apart = jnp.bitwise_and(lax.shift_right_logical(jnp.bitwise_xor(row, col), 2), 1)
    raw = jnp.where(apart * split == 0, raw, 0.0)
    soft = raw / jnp.sum(raw, -1, keepdims=True)
    return q_sum, k_sum, q_len, k_len, q_two, k_unit, scale, soft


def load_out_weights(w_ref, wo_ref):
    for m in range(4):
        for j in range(4):
            wo_ref[m * 128 : m * 128 + 128, j * 128 : j * 128 + 128] = w_ref[
                m, j * 128 : j * 128 + 128, 384:512
            ]


def forward_body(who, scales, x_ref, w_ref, g_ref, hid_ref, mrg_ref, stk_ref, wo_ref, mix_ref):
    split = jnp.where(jnp.logical_and(who[1] == who[3] - 1, who[0] >= 2), 1, 0)
    load_out_weights(w_ref, wo_ref)
    ones = segments()
    x = x_ref[...].astype(F32)
    (center,), scale = norm_parts([x], 512)
    normed = (center * scale).astype(BF)
    for p in range(4):
        stacked = dot(normed, w_ref[p, :, 0:384]).astype(BF)
        stk_ref[p] = stacked
        soft = attend(
            stacked[:, 0:128],
            stacked[:, 128:256],
            scales[2 * p],
            scales[2 * p + 1],
            split,
            ones,
        )[-1].astype(BF)
        values = by_head(stacked[:, 256:384])
        both = jnp.concatenate([soft[0:128], soft[128:256]], 1)
        mix_ref[:, p * 128 : p * 128 + 128] = dot(both, values).astype(BF)
    hidden = (x + dot(mix_ref[...], wo_ref[...])).astype(BF)
    hid_ref[...] = hidden
    parts = [hidden[i * 32 : i * 32 + 32].astype(F32) for i in range(4)]
    centers, scale = norm_parts(parts, 2048)
    for i in range(4):
        piece = (centers[i] * scale).astype(BF)
        for d in range(4):
            mrg_ref[d, 0:32, i * 512 : i * 512 + 512] = piece
    side = lax.shift_right_logical(jnp.bitwise_and(who[0] + 3, 3), 1)
    for d in range(4):
        for j in range(4):
            row = (j // 2) * 64 + d * 16 + (j % 2) * 8
            mrg_ref[d, 32:40, j * 512 : j * 512 + 512] = g_ref[row : row + 8]
            fits = (side == d % 2).astype(F32).astype(BF)
            row = (d // 2) * 64 + j * 16
            mrg_ref[d, 40:56, j * 512 : j * 512 + 512] = g_ref[row : row + 16] * fits


def backward_body(who, scales, x_ref, dh_ref, stk_ref, w_ref, out_ref, wo_ref, acc_ref):
    split = jnp.where(jnp.logical_and(who[1] == who[3] - 1, who[0] >= 2), 1, 0)
    load_out_weights(w_ref, wo_ref)
    ones = segments()
    dh = dh_ref[...]
    for p in range(4):
        stacked = stk_ref[p]
        q, k, v = stacked[:, 0:128], stacked[:, 128:256], stacked[:, 256:384]
        d_mix = dot(dh, wo_ref[p * 128 : p * 128 + 128, :], 1, 1).astype(BF)
        q_sum, k_sum, q_len, k_len, q_two, k_unit, scale, soft = attend(
            q, k, scales[2 * p], scales[2 * p + 1], split, ones
        )
        d_two = by_head(d_mix)
        d_soft = dot(d_two, v, 1, 1).astype(BF).astype(F32)
        d_v = dot(soft.astype(BF), d_two, 0, 0).astype(BF)
        inner = jnp.sum(d_soft * soft, -1, keepdims=True)
        d_score = (soft * (d_soft - inner) * scale).astype(BF)
        both = jnp.concatenate([d_score[0:128], d_score[128:256]], 1)
        d_q = dot(both, by_head(k_unit)).astype(BF).astype(F32)
        d_k = dot(d_score, q_two, 0, 0).astype(BF).astype(F32)

        def unit_back(raw, grad, total, length):
            values = raw.astype(F32)
            share = jnp.where(total > 1.0, 1.0, jnp.where(total == 1.0, 0.5, 0.0))
            along = head_sums(values * grad, ones) * share / jnp.maximum(total, 1.0)
            return ((grad - values * along) / length).astype(BF)

        d_stack = jnp.concatenate(
            [unit_back(q, d_q, q_sum, q_len), unit_back(k, d_k, k_sum, k_len), d_v], 1
        )
        part = dot(d_stack, w_ref[p, :, 0:384], 1, 1)
        if p == 0:
            acc_ref[...] = part
        else:
            acc_ref[...] += part
    d_normed = acc_ref[...].astype(BF).astype(F32)
    (center,), scale = norm_parts([x_ref[...].astype(F32)], 512)
    (d_x,) = norm_back([d_normed], [center], scale, 512)
    grad = (dh.astype(F32) + d_x.astype(BF).astype(F32)).astype(BF)
    send_strips(grad, who[0], out_ref, 0)


def send_strips(window, me, out_ref, at):
    half = jnp.bitwise_and(me, 1)
    for m in range(4):
        strip = (m + 3) % 4
        mine = (half == strip // 2).astype(F32).astype(BF)
        for ab in range(4):
            row = ab * 32 + (strip % 2) * 16
            out_ref[m, at + ab * 16 : at + ab * 16 + 16, :] = window[row : row + 16] * mine


def placed(who, refs):
    x, core = who[4], who[2]
    own, other = refs[0:4], refs[4]
    for step in range(4):
        yield own[step], jnp.bitwise_and(x - STEPS[step], 3), core
        yield other.at[step], jnp.bitwise_and(x - STEPS[step], 3), 1 - core


def merge_body(who, r0, r1, r2, r3, ro, in_ref, mrg_ref, exp_ref, out_ref):
    for ref, x, c in placed(who, (r0, r1, r2, r3, ro)):
        for z in range(2):
            for la in range(4):
                mrg_ref[x, z, c, la * 32 : la * 32 + 32, :] = ref[la, z]
            for la in range(4, 8):
                r = (la % 2) * 32
                n = ((la - 4) // 2) * 256
                exp_ref[x, z, c, r : r + 32, n : n + 256] = ref[la, z]
    blocks = []
    for ih in range(2):
        for strip in range(4):
            for j in range(2 * ih, 2 * ih + 2):
                blocks.append(in_ref[(strip + 1) % 4, 32:40, j * 512 : j * 512 + 512])
    d_exp = jnp.concatenate(blocks, 0)
    d_out = dot(d_exp, exp_ref[...].reshape(1024, 512), 1, 1).astype(BF)
    merged = in_ref[:, 0:32, :].reshape(128, 2048)
    columns = dot(merged, mrg_ref[...].reshape(2048, 256)).astype(BF)
    for d in range(4):
        out_ref[d, :, 0:256] = columns
        out_ref[d, :, 256:1280] = d_out


def dense_body(
    who, r0, r1, r2, r3, ro, in_ref, out_ref, crs_ref, dout_ref, w1_ref, w2_ref
):
    for ref, x, c in placed(who, (r0, r1, r2, r3, ro)):
        for z in range(2):
            for j in range(4):
                w1_ref[x, z, c, :, j * 256 : j * 256 + 256] = ref[j, z]
                w2_ref[x, z, c, :, j * 256 : j * 256 + 256] = ref[j + 4, z]
    w1 = w1_ref[...].reshape(1024, 1024)
    w2 = w2_ref[...].reshape(1024, 1024)
    parts = [in_ref[j, :, 0:256].astype(F32) for j in range(4)]
    centers, scale = norm_parts(parts, 1024)
    for j in range(4):
        crs_ref[:, j * 256 : j * 256 + 256] = in_ref[j, :, 0:256]
    normed = jnp.concatenate([(c * scale).astype(BF) for c in centers], 1)
    d_out = (
        in_ref[0, :, 256:1280].astype(F32)
        + in_ref[1, :, 256:1280].astype(F32)
        + in_ref[2, :, 256:1280].astype(F32)
        + in_ref[3, :, 256:1280].astype(F32)
    ).astype(BF)
    dout_ref[...] = d_out
    inner = dot(normed, w1).astype(BF).astype(F32)
    d_act = dot(d_out, w2).astype(BF).astype(F32)
    rate = 0.7978845608028654
    t = jnp.tanh(rate * (inner + 0.044715 * (inner * inner * inner)))
    share = 0.5 * (1.0 + t)
    act = (inner * share).astype(BF)
    slope = share + 0.5 * inner * (1.0 - t * t) * rate * (1.0 + 0.134145 * (inner * inner))
    d_inner = (d_act * slope).astype(BF)
    d_norm = dot(d_inner, w1, 1, 1).astype(BF)
    outer = dot(act, w2, 1, 1).astype(BF)
    for d in range(4):
        out_ref[d, 0:128] = d_norm
        out_ref[d, 128:160] = outer[d * 32 : d * 32 + 32]


def coarse_back_body(who, recv_ref, crs_ref, dout_ref, w_ref, out_ref, cols_ref):
    me = who[0]
    coarse = crs_ref[...].astype(F32)
    d_norm = (
        recv_ref[0, 0:128].astype(F32)
        + recv_ref[1, 0:128].astype(F32)
        + recv_ref[2, 0:128].astype(F32)
        + recv_ref[3, 0:128].astype(F32)
    )
    d_norm = d_norm.astype(BF).astype(F32)
    (center,), scale = norm_parts([coarse], 1024)
    (d_c,) = norm_back([d_norm], [center], scale, 1024)
    d_coarse = (dout_ref[...].astype(F32) + d_c.astype(BF).astype(F32)).astype(BF)
    for j in range(4):
        cols_ref[j] = d_coarse[:, j * 256 : j * 256 + 256]
    part = dot(cols_ref[me], w_ref[...], 1, 1).astype(BF)
    own = crs_ref[pl.ds(pl.multiple_of(me * 32, 32), 32), :].astype(F32)
    outer = (
        recv_ref[0, 128:160].astype(F32)
        + recv_ref[1, 128:160].astype(F32)
        + recv_ref[2, 128:160].astype(F32)
        + recv_ref[3, 128:160].astype(F32)
    )
    coarse_out = (own + outer).astype(BF)
    for d in range(4):
        out_ref[d, :, 0:2048] = part[d * 32 : d * 32 + 32]
        out_ref[d, :, 2048:3072] = coarse_out


def hidden_back_body(who, recv_ref, hid_ref, g_ref, out_ref):
    half = jnp.bitwise_and(who[0], 1)
    first, second = 2 * half + 1, jnp.bitwise_and(2 * half + 2, 3)
    parts, grads = [], []
    for ab in range(4):
        lanes = slice(ab * 512, ab * 512 + 512)
        total = (
            recv_ref[0, :, lanes].astype(F32)
            + recv_ref[1, :, lanes].astype(F32)
            + recv_ref[2, :, lanes].astype(F32)
            + recv_ref[3, :, lanes].astype(F32)
        )
        grads.append(total.astype(BF).astype(F32))
        parts.append(hid_ref[ab * 32 : ab * 32 + 32].astype(F32))
    centers, scale = norm_parts(parts, 2048)
    back = norm_back(grads, centers, scale, 2048)
    for ab in range(4):
        lanes = slice(ab * 512, ab * 512 + 512)
        for sp, source in ((0, first), (1, second)):
            rows = slice(ab * 32 + sp * 16, ab * 32 + sp * 16 + 16)
            g = g_ref[source, 40:56, lanes].astype(F32)
            b = back[ab][sp * 16 : sp * 16 + 16].astype(BF).astype(F32)
            out_ref[rows, :] = (g + b).astype(BF)


def expand_body(who, recv_ref, hid_ref, w_ref, out_ref):
    coarse_out = recv_ref[:, :, 2048:3072].reshape(128, 1024)
    expanded = dot(coarse_out, w_ref[...]).astype(BF)
    for m in range(4):
        strip = (m + 3) % 4
        for ih in range(2):
            row = (ih * 2 + strip // 2) * 32 + (strip % 2) * 16
            out_ref[m, ih * 16 : ih * 16 + 16, :] = expanded[row : row + 16]
    send_strips(hid_ref[...], who[0], out_ref, 32)


def output_body(who, recv_ref, out_ref):
    half = lax.shift_right_logical(jnp.bitwise_and(who[0] + 3, 3), 1)
    for ih in range(2):
        for ab in range(4):
            hidden = recv_ref[ih * 2 + half, 32 + ab * 16 : 32 + ab * 16 + 16, :]
            added = recv_ref[ab, ih * 16 : ih * 16 + 16, :]
            row = (ih * 4 + ab) * 16
            out_ref[row : row + 16, :] = (hidden.astype(F32) + added.astype(F32)).astype(BF)


def pick(index, source):
    chosen = index[:, None] == jnp.arange(source.shape[0], dtype=jnp.int32)[None]
    return jnp.dot(chosen.astype(BF), source, preferred_element_type=F32).astype(BF)


def grid_of(*sizes):
    return [a.reshape(-1) for a in np.indices(sizes, dtype=np.int32)]


def whole_step(x, qk, wv, wo, scales, w_merge, w_first, w_second, w_expand, g):
    lat = lax.axis_index("lat")
    lats = lax.axis_size("lat")
    core = lax.axis_index("core")
    me = lax.axis_index("mp")
    lons = lax.axis_size(LON)
    who = jnp.stack([me, lat, core, lats, lax.axis_index("x")]).astype(jnp.int32)

    x_flat = x.reshape(512, 512)
    g_flat = g.reshape(128, 512)
    rows = jnp.concatenate(
        [x_flat[0:64], x_flat[256:320], g_flat[0:16], g_flat[64:80]], 0
    )
    rows = lax.ppermute(rows, "lat", [(i, (i - 1) % lats) for i in range(lats)])
    source = jnp.concatenate([x_flat, rows[0:128], g_flat, rows[128:160]], 0)
    ih, a, b, lv, i4, j2 = grid_of(2, 2, 2, 2, 4, 2)
    r, c = ih * 8 + i4 * 2 + a, j2 * 2 + b
    from_g = np.where(r < 12, 640 + lv * 64 + (r + 4) * 4 + c, 768 + lv * 16 + (r - 12) * 4 + c)
    from_x = np.where(r < 12, lv * 256 + (r + 4) * 16 + c, 512 + lv * 64 + (r - 12) * 16 + c)
    sent = pick(jnp.where(me == 0, from_g, from_x), source)
    came = lax.ppermute(sent, LON, [(i, (i - 1) % lons) for i in range(lons)])
    g_strip = jnp.where(me == 0, came, pick(jnp.asarray(from_g), source))
    a, b, sp, lv, i4, j2 = grid_of(2, 2, 2, 2, 4, 2)
    r = (me // 2) * 8 + i4 * 2 + a
    c = 4 + (me % 2) * 8 + sp * 4 + j2 * 2 + b
    near = jnp.where(r < 12, lv * 256 + (r + 4) * 16 + c, 512 + lv * 64 + (r - 12) * 16 + c)
    far = 640 + (me // 2) * 64 + (a * 2 + b) * 16 + lv * 8 + i4 * 2 + j2
    x_win = pick(
        jnp.where(c < 16, near, far), jnp.concatenate([x_flat, rows[0:128], came], 0)
    )

    wo_rows = jnp.concatenate([wo[:, j * 128 : j * 128 + 128] for j in range(4)], 0)
    qkvo = to_all(jnp.concatenate([qk[:, 0], qk[:, 1], wv, wo_rows], 1), "mp")

    def piece(shard):
        n = shard.shape[0] // lats
        return lax.dynamic_slice_in_dim(shard, lat * n, n, 0)

    second = w_second.T
    one = jnp.concatenate([w_merge, w_expand[:, 0:256], w_expand[:, 256:512]], 0)
    two = jnp.concatenate(
        [w[:, j * 256 : j * 256 + 256] for w in (w_first, second) for j in range(4)], 0
    )
    shards = to_all(jnp.concatenate([piece(one), piece(two)], 0), ("lat", "zh"))
    shards = shards.reshape(lats, 2, 96, 256)

    def gathered(own):
        parts = [own]
        for step in STEPS[1:]:
            parts.append(lax.ppermute(own, "x", [(i, (i + step) % 4) for i in range(4)]))
        other = lax.ppermute(jnp.stack(parts), "core", [(0, 1), (1, 0)])
        return (*parts, other)

    one_parts = gathered(shards[:, :, 0:32])
    two_parts = gathered(shards[:, :, 32:96])

    hidden, merged, stacked = call(
        forward_body,
        [arr(128, 512), arr(4, 56, 2048), arr(4, 128, 384)],
        [pltpu.VMEM((512, 512), BF), pltpu.VMEM((128, 512), BF)],
        n_scalar=2,
        n_in=3,
    )(who, scales, x_win, qkvo, g_strip)
    merged = swap(merged, "mp")
    merge_full, expand_full, columns = call(
        merge_body,
        [arr(4, 2, 2, 128, 256), arr(4, 2, 2, 64, 512), arr(4, 128, 1280)],
        n_scalar=1,
        n_in=6,
    )(who, *one_parts, merged)
    merge_full = merge_full.reshape(2048, 256)
    expand_full = expand_full.reshape(1024, 512)
    columns = swap(columns, "mp")
    sums, coarse, d_out = call(
        dense_body,
        [arr(4, 160, 1024), arr(128, 1024), arr(128, 1024)],
        [pltpu.VMEM((4, 2, 2, 64, 1024), BF), pltpu.VMEM((4, 2, 2, 64, 1024), BF)],
        n_scalar=1,
        n_in=6,
    )(who, *two_parts, columns)
    sums = swap(sums, "mp")
    merges = call(
        coarse_back_body,
        arr(4, 32, 3072),
        [pltpu.VMEM((4, 128, 256), BF)],
        n_scalar=1,
        n_in=4,
    )(who, sums, coarse, d_out, merge_full)
    merges = swap(merges, "mp")
    d_hidden = call(hidden_back_body, arr(128, 512), n_scalar=1, n_in=3)(
        who, merges, hidden, merged
    )
    grads = call(
        backward_body,
        arr(4, 64, 512),
        [pltpu.VMEM((512, 512), BF), pltpu.VMEM((128, 512), F32)],
        n_scalar=2,
        n_in=4,
    )(who, scales, x_win, d_hidden, stacked, qkvo)
    grads = swap(grads, "mp")
    added = call(expand_body, arr(4, 96, 512), n_scalar=1, n_in=3)(
        who, merges, hidden, expand_full
    )
    added = swap(added, "mp")
    out_strip = call(output_body, arr(128, 512), n_scalar=1, n_in=1)(who, added)
    half = ((me + 3) % 4) // 2
    grad_strip = jnp.concatenate(
        [
            lax.dynamic_index_in_dim(grads, half, 0, False),
            lax.dynamic_index_in_dim(grads, half + 2, 0, False),
        ],
        0,
    )

    across = [(lon * 4, ((lon + 1) % lons) * 4) for lon in range(lons)]
    down = [
        ((la * lons + lon) * 4 + m, (((la + 1) % lats) * lons + (lon + (m == 0)) % lons) * 4 + m)
        for la in range(lats)
        for lon in range(lons)
        for m in range(4)
    ]
    lv, r, c = grid_of(2, 16, 4)
    s = r - 4
    kept = (s // 8) * 64 + ((s % 2) * 2 + c % 2) * 16 + lv * 8 + ((s % 8) // 2) * 2 + c // 2
    tops = np.where(
        r < 4, 256 + ((r % 2) * 2 + c % 2) * 8 + lv * 4 + (r // 2) * 2 + c // 2, 0
    )

    def rolled_back(strip):
        beyond = lax.ppermute(strip, LONMP, across)
        last = strip[64:128].reshape(8, 8, 512)[:, 4:8].reshape(32, 512)
        above = lax.ppermute(last, ALL, down)
        shift = jnp.where(me == 0, 128, 0)
        index = jnp.where(r < 4, tops, kept + shift)
        whole = pick(index, jnp.concatenate([strip, beyond, above], 0))
        return whole.reshape(2, 16, 4, 512)

    return rolled_back(out_strip), rolled_back(grad_strip)


def solution(mesh):
    lats, lons, mps = (mesh.shape[n] for n in ("lat", "lon", "mp"))
    fine = Mesh(
        mesh.devices.reshape(lats, lons // 4, 2, 2, mps), ("lat", "x", "zh", "core", "mp")
    )
    in_specs = (
        P(None, "lat", LON, None),
        P(None, None, "mp"),
        P(None, "mp"),
        P("mp", None),
        P(),
        P(LON, "mp"),
        P(LON, "mp"),
        P("mp", LON),
        P(LON, "mp"),
        P(None, "lat", LONMP, None),
    )
    out_specs = (P(None, "lat", LONMP, None), P(None, "lat", LONMP, None))
    return jax.shard_map(
        whole_step, mesh=fine, in_specs=in_specs, out_specs=out_specs, check_vma=False
    )
```

profile of v0, /device:TPU:6, one launch (start us, length us, event | category | flops | bytes accessed | tf_op | source)
XLA Modules:
  0.0 262.7 jit_solution(10185693530062255390)
XLA Ops:
  9.3 15.2 %all-to-all-start = ((bf16[16,96,256]{2,1,0:T(8,128)(2,1)}), bf16[16,96,256]{2,1,0:T(8,128)(2,1)S(1)}, u32[]{:S(2)}, u32[]{:S(2)}) async-start(bf16[16,96,256]{2,1,0:T(8,128)(2,1)} %broadcast_in_dim.4), calls=%async_computation | async-start | bytes 1572864 | tf_op jit(solution)/shard_map/all_to_all | solution.py:23
  26.2 10.4 %collective-permute-start.8 = (bf16[160,512]{1,0:T(8,128)(2,1)}, bf16[160,512]{1,0:T(8,128)(2,1)}, u32[]{:S(2)}, u32[]{:S(2)}) collective-permute-start(bf16[160,512]{1,0:T(8,128)(2,1)} %pad_maximum_fusion.3), channel_id=1, source_target_pairs={{0,448},{64,0},{128,64},{192,128},{256,192},{320,256},{384,320},{4... | collective-permute-start | bytes 491528 | tf_op jit(solution)/shard_map/ppermute | solution.py:367
  37.2 30.6 %all-to-all-done = bf16[16,96,256]{2,1,0:T(8,128)(2,1)S(1)} async-done(((bf16[16,96,256]{2,1,0:T(8,128)(2,1)}), bf16[16,96,256]{2,1,0:T(8,128)(2,1)S(1)}, u32[]{:S(2)}, u32[]{:S(2)}) %all-to-all-start) | async-done | bytes 786464 | tf_op jit(solution)/shard_map/all_to_all | solution.py:23
  69.5 4.6 %all-to-all-start.1 = ((bf16[4,512,512]{2,1,0:T(8,128)(2,1)}), bf16[4,512,512]{2,1,0:T(8,128)(2,1)S(1)}, u32[]{:S(2)}, u32[]{:S(2)}) async-start(bf16[4,512,512]{2,1,0:T(8,128)(2,1)} %broadcast_in_dim.5), calls=%async_computation.1 | async-start | bytes 4194304 | tf_op jit(solution)/shard_map/all_to_all | solution.py:23
  74.9 2.4 collective-permute-start.4
  79.2 3.4 %collective-permute-start = (bf16[8,2,64,256]{3,2,1,0:T(8,128)(2,1)S(1)}, bf16[8,2,64,256]{3,2,1,0:T(8,128)(2,1)S(1)}, u32[]{:S(2)}, u32[]{:S(2)}) collective-permute-start(bf16[8,2,64,256]{3,2,1,0:T(8,128)(2,1)S(1)} %get-tuple-element.23.r0), channel_id=1, source_target_pairs={{0,16},{16,32},{32,48},{48,0},{1,17},{17,33},{33,49},{49,1},{2,18}... | collective-permute-start | bytes 1572872 | tf_op jit(solution)/shard_map/ppermute | solution.py:403
  82.6 2.4 collective-permute-start.1
  85.1 4.3 %collective-permute-start.2 = (bf16[8,2,64,256]{3,2,1,0:T(8,128)(2,1)S(1)}, bf16[8,2,64,256]{3,2,1,0:T(8,128)(2,1)}, u32[]{:S(2)}, u32[]{:S(2)}) collective-permute-start(bf16[8,2,64,256]{3,2,1,0:T(8,128)(2,1)S(1)} %get-tuple-element.23.r0), channel_id=1, source_target_pairs={{0,32},{16,48},{32,0},{48,16},{1,33},{17,49},{33,1},{49,17},{2,34}... | collective-permute-start | bytes 1572872 | tf_op jit(solution)/shard_map/ppermute | solution.py:403
  89.4 3.0 %collective-permute-start.5 = (bf16[8,2,32,256]{3,2,1,0:T(8,128)(2,1)S(1)}, bf16[8,2,32,256]{3,2,1,0:T(8,128)(2,1)}, u32[]{:S(2)}, u32[]{:S(2)}) collective-permute-start(bf16[8,2,32,256]{3,2,1,0:T(8,128)(2,1)S(1)} %get-tuple-element.21.r0), channel_id=1, source_target_pairs={{0,48},{16,0},{32,16},{48,32},{1,49},{17,1},{33,17},{49,33},{2,50}... | collective-permute-start | bytes 786440 | tf_op jit(solution)/shard_map/ppermute | solution.py:403
  92.5 4.0 %collective-permute-start.6 = (bf16[8,2,32,256]{3,2,1,0:T(8,128)(2,1)S(1)}, bf16[8,2,32,256]{3,2,1,0:T(8,128)(2,1)}, u32[]{:S(2)}, u32[]{:S(2)}) collective-permute-start(bf16[8,2,32,256]{3,2,1,0:T(8,128)(2,1)S(1)} %get-tuple-element.21.r0), channel_id=1, source_target_pairs={{0,32},{16,48},{32,0},{48,16},{1,33},{17,49},{33,1},{49,17},{2,34}... | collective-permute-start | bytes 786440 | tf_op jit(solution)/shard_map/ppermute | solution.py:403
  100.3 17.7 %collective-permute-done.5.r2 = bf16[8,2,32,256]{3,2,1,0:T(8,128)(2,1)} collective-permute-done((bf16[8,2,32,256]{3,2,1,0:T(8,128)(2,1)S(1)}, bf16[8,2,32,256]{3,2,1,0:T(8,128)(2,1)}, u32[]{:S(2)}, u32[]{:S(2)}) %collective-permute-start.5) | collective-permute-done | bytes 262176 | tf_op jit(solution)/shard_map/ppermute | solution.py:403
  119.9 2.3 pad_maximum_fusion.1
  122.2 2.4 collective-permute-start.7
  124.7 2.9 %pad_maximum_fusion = bf16[4,8,2,64,256]{4,3,2,1,0:T(8,128)(2,1)} fusion(bf16[1,8,2,64,256]{4,3,2,1,0:T(8,128)(2,1)} %bitcast.9, bf16[1,8,2,64,256]{4,3,2,1,0:T(8,128)(2,1)} %bitcast.8, bf16[1,8,2,64,256]{4,3,2,1,0:T(8,128)(2,1)S(1)} %bitcast.31, bf16[1,8,2,64,256]{4,3,2,1,0:T(8,128)(2,1)S(1)} %copy-done.7), kind=kLoop, calls=%fused_computation | loop fusion | flops 3145728 | bytes 4194304 | tf_op jit(solution)/shard_map/stack | solution.py:404
  127.6 2.0 collective-permute-start.3
  131.9 3.8 %shard_map.266 = (bf16[128,512]{1,0:T(8,128)(2,1)S(1)}, bf16[4,56,2048]{2,1,0:T(8,128)(2,1)S(1)}, bf16[4,128,384]{2,1,0:T(8,128)(2,1)S(1)}) custom-call(s32[5]{0:T(128)S(1)} %stack.49.who, f32[8]{0:T(128)S(1)} %copy-done.5, bf16[128,512]{1,0:T(8,128)(2,1)S(1)} %convolution_convert_fusion.1.x_ref, bf16[4,512,512]{2,1,0:T(8,128)(2,1)S(1)} %all-to-all-done.1.w_ref, ...), custom_call_target="tpu_custom_call" | custom-call | tf_op jit(solution)/shard_map/pallas_call | solution.py:410
  135.8 18.7 %all_to_all.40.in_ref.g_ref = bf16[4,56,2048]{2,1,0:T(8,128)(2,1)S(1)} all-to-all(bf16[4,56,2048]{2,1,0:T(8,128)(2,1)S(1)} %get-tuple-element.11), channel_id=1, replica_groups=mesh['lat'=8,'x'=4,'zh'=2,'core'=2,'mp'=4] {'mp'}, dimensions={0} | all-to-all | bytes 1835008 | tf_op jit(solution)/shard_map/all_to_all | solution.py:29
  154.4 2.2 shard_map.267
  157.6 20.1 %all_to_all.41.in_ref = bf16[4,128,1280]{2,1,0:T(8,128)(2,1)S(1)} all-to-all(bf16[4,128,1280]{2,1,0:T(8,128)(2,1)S(1)} %get-tuple-element.12), channel_id=1, replica_groups=mesh['lat'=8,'x'=4,'zh'=2,'core'=2,'mp'=4] {'mp'}, dimensions={0} | all-to-all | bytes 2621440 | tf_op jit(solution)/shard_map/all_to_all | solution.py:29
  177.8 4.6 %shard_map.268 = (bf16[4,160,1024]{2,1,0:T(8,128)(2,1)S(1)}, bf16[128,1024]{1,0:T(8,128)(2,1)S(1)}, bf16[128,1024]{1,0:T(8,128)(2,1)S(1)}) custom-call(s32[5]{0:T(128)S(1)} %stack.49.who, bf16[8,2,64,256]{3,2,1,0:T(8,128)(2,1)S(1)} %get-tuple-element.23.r0, bf16[8,2,64,256]{3,2,1,0:T(8,128)(2,1)S(1)} %collective-permute-done.r1, ...), custom_call_target="tpu_custom_call" | custom-call | tf_op jit(solution)/shard_map/pallas_call | solution.py:427
  182.4 19.3 %all_to_all.42.recv_ref = bf16[4,160,1024]{2,1,0:T(8,128)(2,1)S(1)} all-to-all(bf16[4,160,1024]{2,1,0:T(8,128)(2,1)S(1)} %get-tuple-element.13), channel_id=1, replica_groups=mesh['lat'=8,'x'=4,'zh'=2,'core'=2,'mp'=4] {'mp'}, dimensions={0} | all-to-all | bytes 2621440 | tf_op jit(solution)/shard_map/all_to_all | solution.py:29
  203.2 12.5 %all_to_all.43.recv_ref = bf16[4,32,3072]{2,1,0:T(8,128)(2,1)S(1)} all-to-all(bf16[4,32,3072]{2,1,0:T(8,128)(2,1)S(1)} %shard_map.269), channel_id=1, replica_groups=mesh['lat'=8,'x'=4,'zh'=2,'core'=2,'mp'=4] {'mp'}, dimensions={0} | all-to-all | bytes 1572864 | tf_op jit(solution)/shard_map/all_to_all | solution.py:29
  216.6 5.4 %shard_map.273 = bf16[4,64,512]{2,1,0:T(8,128)(2,1)} custom-call(s32[5]{0:T(128)S(1)} %stack.49.who, f32[8]{0:T(128)S(1)} %copy-done.5, bf16[128,512]{1,0:T(8,128)(2,1)S(1)} %convolution_convert_fusion.1.x_ref, bf16[128,512]{1,0:T(8,128)(2,1)S(1)} %shard_map.272.dh_ref, bf16[4,128,384]{2,1,0:T(8,128)(2,1)S(1)} %get-tuple-element.19.stk_ref, ...), custom_call_target="tpu_custom_call" | custom-call | tf_op jit(solution)/shard_map/pallas_call | solution.py:446
  222.0 3.4 %all-to-all-start.7 = ((bf16[4,64,512]{2,1,0:T(8,128)(2,1)}), bf16[4,64,512]{2,1,0:T(8,128)(2,1)S(1)}, u32[]{:S(2)}, u32[]{:S(2)}) async-start(bf16[4,64,512]{2,1,0:T(8,128)(2,1)} %shard_map.273), calls=%async_computation.7 | async-start | bytes 524288 | tf_op jit(solution)/shard_map/all_to_all | solution.py:29
  228.3 3.7 %all-to-all-done.7 = bf16[4,64,512]{2,1,0:T(8,128)(2,1)S(1)} async-done(((bf16[4,64,512]{2,1,0:T(8,128)(2,1)}), bf16[4,64,512]{2,1,0:T(8,128)(2,1)S(1)}, u32[]{:S(2)}, u32[]{:S(2)}) %all-to-all-start.7) | async-done | bytes 262176 | tf_op jit(solution)/shard_map/all_to_all | solution.py:29
  232.1 3.5 %all-to-all-start.6 = ((bf16[4,96,512]{2,1,0:T(8,128)(2,1)}), bf16[4,96,512]{2,1,0:T(8,128)(2,1)S(1)}, u32[]{:S(2)}, u32[]{:S(2)}) async-start(bf16[4,96,512]{2,1,0:T(8,128)(2,1)} %shard_map.270), calls=%async_computation.6 | async-start | bytes 786432 | tf_op jit(solution)/shard_map/all_to_all | solution.py:29
  235.7 1.9 collective-permute-start.13
  237.7 7.3 %collective-permute-start.12 = (bf16[128,512]{1,0:T(8,128)(2,1)S(1)}, bf16[128,512]{1,0:T(8,128)(2,1)S(1)}, u32[]{:S(2)}, u32[]{:S(2)}) collective-permute-start(bf16[128,512]{1,0:T(8,128)(2,1)S(1)} %pad_maximum_fusion.6), channel_id=1, source_target_pairs={{0,4},{4,8},{8,12},{12,16},{16,20},{20,24},{24,28},{28,32},{32,36}... | collective-permute-start | bytes 393224 | tf_op jit(solution)/shard_map/ppermute | solution.py:483
  245.6 1.9 collective-permute-start.10
  247.6 6.3 %collective-permute-start.11 = (bf16[32,512]{1,0:T(8,128)(2,1)S(1)}, bf16[32,512]{1,0:T(8,128)(2,1)S(1)}, u32[]{:S(2)}, u32[]{:S(2)}) collective-permute-start(bf16[32,512]{1,0:T(8,128)(2,1)S(1)} %reshape.51), channel_id=1, source_target_pairs={{0,68},{1,65},{2,66},{3,67},{4,72},{5,69},{6,70},{7,71},{8,76},{9,... | collective-permute-start | bytes 98312 | tf_op jit(solution)/shard_map/ppermute | solution.py:485
  254.9 4.4 %collective-permute-done.11 = bf16[32,512]{1,0:T(8,128)(2,1)S(1)} collective-permute-done((bf16[32,512]{1,0:T(8,128)(2,1)S(1)}, bf16[32,512]{1,0:T(8,128)(2,1)S(1)}, u32[]{:S(2)}, u32[]{:S(2)}) %collective-permute-start.11) | collective-permute-done | bytes 32800 | tf_op jit(solution)/shard_map/ppermute | solution.py:485
  259.3 2.4 collective-permute-done.10
  (114 shorter events, 32.0 us)
Async XLA Ops:
  2.2 22.4 %copy-start.12 = (bf16[2,16,4,512]{3,2,1,0:T(4,128)(2,1)S(1)}, bf16[2,16,4,512]{3,2,1,0:T(4,128)(2,1)}, u32[]{:S(2)}) copy-start(bf16[2,16,4,512]{3,2,1,0:T(4,128)(2,1)} %param.36) | copy-start | bytes 393220
  8.3 28.4 %copy-start.13 = (bf16[128,512]{1,0:T(8,128)(2,1)S(1)}, bf16[128,512]{1,0:T(8,128)(2,1)}, u32[]{:S(2)}) copy-start(bf16[128,512]{1,0:T(8,128)(2,1)} %param.30) | copy-start | bytes 393220
  8.3 28.4 %copy-start.8 = (bf16[512,2,128]{2,1,0:T(2,128)(2,1)S(1)}, bf16[512,2,128]{2,1,0:T(2,128)(2,1)}, u32[]{:S(2)}) copy-start(bf16[512,2,128]{2,1,0:T(2,128)(2,1)} %param.28) | copy-start | bytes 786436
  9.3 58.5 %all-to-all-start = ((bf16[16,96,256]{2,1,0:T(8,128)(2,1)}), bf16[16,96,256]{2,1,0:T(8,128)(2,1)S(1)}, u32[]{:S(2)}, u32[]{:S(2)}) async-start(bf16[16,96,256]{2,1,0:T(8,128)(2,1)} %broadcast_in_dim.4), calls=%async_computation | async-start | bytes 1572864 | tf_op jit(solution)/shard_map/all_to_all | solution.py:23
  24.6 12.6 %copy-start.14 = (bf16[512,128]{1,0:T(8,128)(2,1)S(1)}, bf16[512,128]{1,0:T(8,128)(2,1)}, u32[]{:S(2)}) copy-start(bf16[512,128]{1,0:T(8,128)(2,1)} %param.29) | copy-start | bytes 393220
  24.6 74.3 %copy-start.10 = (bf16[128,512]{1,0:T(8,128)(2,1)}, bf16[128,512]{1,0:T(8,128)(2,1)S(1)}, u32[]{:S(2)}) copy-start(bf16[128,512]{1,0:T(8,128)(2,1)S(1)} %reshape.47) | copy-start | bytes 393220
  26.2 63.2 %collective-permute-start.8 = (bf16[160,512]{1,0:T(8,128)(2,1)}, bf16[160,512]{1,0:T(8,128)(2,1)}, u32[]{:S(2)}, u32[]{:S(2)}) collective-permute-start(bf16[160,512]{1,0:T(8,128)(2,1)} %pad_maximum_fusion.3), channel_id=1, source_target_pairs={{0,448},{64,0},{128,64},{192,128},{256,192},{320,256},{384,320},{4... | collective-permute-start | bytes 491528 | tf_op jit(solution)/shard_map/ppermute | solution.py:367
  69.5 61.5 %all-to-all-start.1 = ((bf16[4,512,512]{2,1,0:T(8,128)(2,1)}), bf16[4,512,512]{2,1,0:T(8,128)(2,1)S(1)}, u32[]{:S(2)}, u32[]{:S(2)}) async-start(bf16[4,512,512]{2,1,0:T(8,128)(2,1)} %broadcast_in_dim.5), calls=%async_computation.1 | async-start | bytes 4194304 | tf_op jit(solution)/shard_map/all_to_all | solution.py:23
  74.1 22.4 %copy-start.24 = (s32[128]{0:T(128)S(1)}, s32[128]{0:T(128)}, u32[]{:S(2)}) copy-start(s32[128]{0:T(128)} %constant.125.clone) | copy-start | bytes 1540
  74.1 22.4 %copy-start.25 = (s32[128]{0:T(128)S(1)}, s32[128]{0:T(128)}, u32[]{:S(2)}) copy-start(s32[128]{0:T(128)} %constant.126.clone) | copy-start | bytes 1540
  74.9 17.6 %collective-permute-start.4 = (bf16[8,2,32,256]{3,2,1,0:T(8,128)(2,1)S(1)}, bf16[8,2,32,256]{3,2,1,0:T(8,128)(2,1)}, u32[]{:S(2)}, u32[]{:S(2)}) collective-permute-start(bf16[8,2,32,256]{3,2,1,0:T(8,128)(2,1)S(1)} %get-tuple-element.21.r0), channel_id=1, source_target_pairs={{0,16},{16,32},{32,48},{48,0},{1,17},{17,33},{33,49},{49,1},{2,18}... | collective-permute-start | bytes 786440 | tf_op jit(solution)/shard_map/ppermute | solution.py:403
  79.2 45.4 %collective-permute-start = (bf16[8,2,64,256]{3,2,1,0:T(8,128)(2,1)S(1)}, bf16[8,2,64,256]{3,2,1,0:T(8,128)(2,1)S(1)}, u32[]{:S(2)}, u32[]{:S(2)}) collective-permute-start(bf16[8,2,64,256]{3,2,1,0:T(8,128)(2,1)S(1)} %get-tuple-element.23.r0), channel_id=1, source_target_pairs={{0,16},{16,32},{32,48},{48,0},{1,17},{17,33},{33,49},{49,1},{2,18}... | collective-permute-start | bytes 1572872 | tf_op jit(solution)/shard_map/ppermute | solution.py:403
  82.6 42.0 %collective-permute-start.1 = (bf16[8,2,64,256]{3,2,1,0:T(8,128)(2,1)S(1)}, bf16[8,2,64,256]{3,2,1,0:T(8,128)(2,1)}, u32[]{:S(2)}, u32[]{:S(2)}) collective-permute-start(bf16[8,2,64,256]{3,2,1,0:T(8,128)(2,1)S(1)} %get-tuple-element.23.r0), channel_id=1, source_target_pairs={{0,48},{16,0},{32,16},{48,32},{1,49},{17,1},{33,17},{49,33},{2,50}... | collective-permute-start | bytes 1572872 | tf_op jit(solution)/shard_map/ppermute | solution.py:403
  85.1 39.6 %collective-permute-start.2 = (bf16[8,2,64,256]{3,2,1,0:T(8,128)(2,1)S(1)}, bf16[8,2,64,256]{3,2,1,0:T(8,128)(2,1)}, u32[]{:S(2)}, u32[]{:S(2)}) collective-permute-start(bf16[8,2,64,256]{3,2,1,0:T(8,128)(2,1)S(1)} %get-tuple-element.23.r0), channel_id=1, source_target_pairs={{0,32},{16,48},{32,0},{48,16},{1,33},{17,49},{33,1},{49,17},{2,34}... | collective-permute-start | bytes 1572872 | tf_op jit(solution)/shard_map/ppermute | solution.py:403
  89.4 28.6 %collective-permute-start.5 = (bf16[8,2,32,256]{3,2,1,0:T(8,128)(2,1)S(1)}, bf16[8,2,32,256]{3,2,1,0:T(8,128)(2,1)}, u32[]{:S(2)}, u32[]{:S(2)}) collective-permute-start(bf16[8,2,32,256]{3,2,1,0:T(8,128)(2,1)S(1)} %get-tuple-element.21.r0), channel_id=1, source_target_pairs={{0,48},{16,0},{32,16},{48,32},{1,49},{17,1},{33,17},{49,33},{2,50}... | collective-permute-start | bytes 786440 | tf_op jit(solution)/shard_map/ppermute | solution.py:403
  92.5 27.4 %collective-permute-start.6 = (bf16[8,2,32,256]{3,2,1,0:T(8,128)(2,1)S(1)}, bf16[8,2,32,256]{3,2,1,0:T(8,128)(2,1)}, u32[]{:S(2)}, u32[]{:S(2)}) collective-permute-start(bf16[8,2,32,256]{3,2,1,0:T(8,128)(2,1)S(1)} %get-tuple-element.21.r0), channel_id=1, source_target_pairs={{0,32},{16,48},{32,0},{48,16},{1,33},{17,49},{33,1},{49,17},{2,34}... | collective-permute-start | bytes 786440 | tf_op jit(solution)/shard_map/ppermute | solution.py:403
  98.9 21.1 %copy-start.9 = (bf16[1,8,2,32,256]{4,3,2,1,0:T(8,128)(2,1)S(1)}, bf16[1,8,2,32,256]{4,3,2,1,0:T(8,128)(2,1)}, u32[]{:S(2)}) copy-start(bf16[1,8,2,32,256]{4,3,2,1,0:T(8,128)(2,1)} %get-tuple-element.20) | copy-start | bytes 786436
  100.3 24.4 %copy-start.7 = (bf16[1,8,2,64,256]{4,3,2,1,0:T(8,128)(2,1)S(1)}, bf16[1,8,2,64,256]{4,3,2,1,0:T(8,128)(2,1)}, u32[]{:S(2)}) copy-start(bf16[1,8,2,64,256]{4,3,2,1,0:T(8,128)(2,1)} %get-tuple-element.22) | copy-start | bytes 1572868
  118.0 11.6 %collective-permute-start.9 = (bf16[128,512]{1,0:T(8,128)(2,1)S(1)}, bf16[128,512]{1,0:T(8,128)(2,1)S(1)}, u32[]{:S(2)}, u32[]{:S(2)}) collective-permute-start(bf16[128,512]{1,0:T(8,128)(2,1)S(1)} %convolution_convert_fusion.2), channel_id=1, source_target_pairs={{0,60},{4,0},{8,4},{12,8},{16,12},{20,16},{24,20},{28,24},{32,28},... | collective-permute-start | bytes 393224 | tf_op jit(solution)/shard_map/ppermute | solution.py:374
  122.2 32.2 %collective-permute-start.7 = (bf16[4,8,2,32,256]{4,3,2,1,0:T(8,128)(2,1)}, bf16[4,8,2,32,256]{4,3,2,1,0:T(8,128)(2,1)}, u32[]{:S(2)}, u32[]{:S(2)}) collective-permute-start(bf16[4,8,2,32,256]{4,3,2,1,0:T(8,128)(2,1)} %pad_maximum_fusion.1), channel_id=1, source_target_pairs={{0,4},{4,0},{1,5},{5,1},{2,6},{6,2},{3,7},{7,3},{8,12},{12,8},{9,1... | collective-permute-start | bytes 3145736 | tf_op jit(solution)/shard_map/ppermute | solution.py:404
  127.6 50.2 %collective-permute-start.3 = (bf16[4,8,2,64,256]{4,3,2,1,0:T(8,128)(2,1)}, bf16[4,8,2,64,256]{4,3,2,1,0:T(8,128)(2,1)}, u32[]{:S(2)}, u32[]{:S(2)}) collective-permute-start(bf16[4,8,2,64,256]{4,3,2,1,0:T(8,128)(2,1)} %pad_maximum_fusion), channel_id=1, source_target_pairs={{0,4},{4,0},{1,5},{5,1},{2,6},{6,2},{3,7},{7,3},{8,12},{12,8},{9,1... | collective-permute-start | bytes 6291464 | tf_op jit(solution)/shard_map/ppermute | solution.py:404
  135.8 79.9 %copy-start.2 = (bf16[128,512]{1,0:T(8,128)(2,1)}, bf16[128,512]{1,0:T(8,128)(2,1)S(1)}, u32[]{:S(2)}) copy-start(bf16[128,512]{1,0:T(8,128)(2,1)S(1)} %get-tuple-element.17.hid_ref) | copy-start | bytes 393220
  216.6 8.9 %copy-start.3 = (bf16[128,512]{1,0:T(8,128)(2,1)S(1)}, bf16[128,512]{1,0:T(8,128)(2,1)}, u32[]{:S(2)}) copy-start(bf16[128,512]{1,0:T(8,128)(2,1)} %copy-done.2) | copy-start | bytes 393220
  222.0 10.1 %all-to-all-start.7 = ((bf16[4,64,512]{2,1,0:T(8,128)(2,1)}), bf16[4,64,512]{2,1,0:T(8,128)(2,1)S(1)}, u32[]{:S(2)}, u32[]{:S(2)}) async-start(bf16[4,64,512]{2,1,0:T(8,128)(2,1)} %shard_map.273), calls=%async_computation.7 | async-start | bytes 524288 | tf_op jit(solution)/shard_map/all_to_all | solution.py:29
  225.4 10.1 %copy-start.16 = (pred[128]{0:T(512)(128)(4,1)S(1)}, pred[128]{0:T(512)(128)(4,1)}, u32[]{:S(2)}) copy-start(pred[128]{0:T(512)(128)(4,1)} %constant.138.clone) | copy-start | bytes 388
  225.4 10.1 %copy-start.17 = (s32[128]{0:T(128)S(1)}, s32[128]{0:T(128)}, u32[]{:S(2)}) copy-start(s32[128]{0:T(128)} %constant.139.clone) | copy-start | bytes 1540
  225.5 10.1 %copy-start.18 = (s32[128]{0:T(128)S(1)}, s32[128]{0:T(128)}, u32[]{:S(2)}) copy-start(s32[128]{0:T(128)} %constant.137.clone) | copy-start | bytes 1540
  232.1 12.9 %all-to-all-start.6 = ((bf16[4,96,512]{2,1,0:T(8,128)(2,1)}), bf16[4,96,512]{2,1,0:T(8,128)(2,1)S(1)}, u32[]{:S(2)}, u32[]{:S(2)}) async-start(bf16[4,96,512]{2,1,0:T(8,128)(2,1)} %shard_map.270), calls=%async_computation.6 | async-start | bytes 786432 | tf_op jit(solution)/shard_map/all_to_all | solution.py:29
  235.7 18.2 %collective-permute-start.13 = (bf16[32,512]{1,0:T(8,128)(2,1)S(1)}, bf16[32,512]{1,0:T(8,128)(2,1)S(1)}, u32[]{:S(2)}, u32[]{:S(2)}) collective-permute-start(bf16[32,512]{1,0:T(8,128)(2,1)S(1)} %reshape.54), channel_id=1, source_target_pairs={{0,68},{1,65},{2,66},{3,67},{4,72},{5,69},{6,70},{7,71},{8,76},{9,... | collective-permute-start | bytes 98312 | tf_op jit(solution)/shard_map/ppermute | solution.py:485
  237.7 16.2 %collective-permute-start.12 = (bf16[128,512]{1,0:T(8,128)(2,1)S(1)}, bf16[128,512]{1,0:T(8,128)(2,1)S(1)}, u32[]{:S(2)}, u32[]{:S(2)}) collective-permute-start(bf16[128,512]{1,0:T(8,128)(2,1)S(1)} %pad_maximum_fusion.6), channel_id=1, source_target_pairs={{0,4},{4,8},{8,12},{12,16},{16,20},{20,24},{24,28},{28,32},{32,36}... | collective-permute-start | bytes 393224 | tf_op jit(solution)/shard_map/ppermute | solution.py:483
  245.6 16.1 %collective-permute-start.10 = (bf16[128,512]{1,0:T(8,128)(2,1)S(1)}, bf16[128,512]{1,0:T(8,128)(2,1)S(1)}, u32[]{:S(2)}, u32[]{:S(2)}) collective-permute-start(bf16[128,512]{1,0:T(8,128)(2,1)S(1)} %shard_map.271), channel_id=1, source_target_pairs={{0,4},{4,8},{8,12},{12,16},{16,20},{20,24},{24,28},{28,32},{32,36}... | collective-permute-start | bytes 393224 | tf_op jit(solution)/shard_map/ppermute | solution.py:483
  247.6 11.7 %collective-permute-start.11 = (bf16[32,512]{1,0:T(8,128)(2,1)S(1)}, bf16[32,512]{1,0:T(8,128)(2,1)S(1)}, u32[]{:S(2)}, u32[]{:S(2)}) collective-permute-start(bf16[32,512]{1,0:T(8,128)(2,1)S(1)} %reshape.51), channel_id=1, source_target_pairs={{0,68},{1,65},{2,66},{3,67},{4,72},{5,69},{6,70},{7,71},{8,76},{9,... | collective-permute-start | bytes 98312 | tf_op jit(solution)/shard_map/ppermute | solution.py:485
  (12 other events, 56.7 us)
where the time goes:
time: 267 us; the launch traced here: 263 us
  starting transfers between devices  80.5 us (30%)
  blocking collectives  70.6 us (26%)
  waiting for transfers between devices  59 us (22%)
  Pallas kernels  20.6 us (8%)
  local copies, waits for them, and re-layouts  20 us (7%)
  other arithmetic  7.25 us (3%)
  matrix products  3.28 us (1%)
    all_to_all x4, blocking collectives, swap(): return lax.all_to_all(value, axis, 0, 0, tiled=True)  70.6 us
    all_to_all x2, waiting for transfers between devices, to_all(): lax.all_to_all(jnp.broadcast_to(value[None], (n, *value.shape)), axis, 0,...  30.6 us
    all_to_all x2, starting transfers between devices, to_all(): lax.all_to_all(jnp.broadcast_to(value[None], (n, *value.shape)), axis, 0,...  19.8 us
    ppermute x6, starting transfers between devices, gathered(): lax.ppermute(own, 'x', [(i, (i + step) % 4) for i in range(4)])  19.6 us
    ppermute x6, waiting for transfers between devices, gathered(): lax.ppermute(own, 'x', [(i, (i + step) % 4) for i in range(4)])  17.7 us
    ppermute x1, starting transfers between devices, whole_step(): rows = lax.ppermute(rows, 'lat', [(i, (i - 1) % lats) for i in range(lats)])  10.4 us
    ppermute x2, starting transfers between devices, rolled_back(): beyond = lax.ppermute(strip, LONMP, across)  9.26 us
    unnamed x59, local copies, waits for them, and re-layouts  8.62 us
  transfers between devices with their start and end apart: 18, of which 5 were waited for; matrix products, arithmetic and copies ran while one was open for 7% of the time, Pallas kernels for 3%

commit v1 on v0

--- a/solution.py
+++ b/solution.py
@@ -18,23 +18,14 @@
     return lax.dot_general(a, b, (((ca,), (cb,)), ((), ())), preferred_element_type=F32)
 
 
-def to_all(value, axis):
-    n = lax.axis_size(axis)
-    return lax.all_to_all(
-        jnp.broadcast_to(value[None], (n, *value.shape)), axis, 0, 0, tiled=True
-    )
-
-
 def swap(value, axis):
     return lax.all_to_all(value, axis, 0, 0, tiled=True)
 
 
 def call(body, outs, scratch=(), n_scalar=0, n_in=0):
-    specs = [pl.BlockSpec(memory_space=pltpu.SMEM)] * n_scalar + [
-        pl.BlockSpec(memory_space=pltpu.VMEM)
-    ] * n_in
+    specs = [pl.BlockSpec(memory_space=pltpu.SMEM)] * n_scalar + [pl.BlockSpec()] * n_in
     many = isinstance(outs, (list, tuple))
-    ospecs = [pl.BlockSpec(memory_space=pltpu.VMEM)] * (len(outs) if many else 1)
+    ospecs = [pl.BlockSpec()] * (len(outs) if many else 1)
     return pl.pallas_call(
         body,
         out_shape=outs,
@@ -100,24 +91,50 @@
     return q_sum, k_sum, q_len, k_len, q_two, k_unit, scale, soft
 
 
-def load_out_weights(w_ref, wo_ref):
-    for m in range(4):
+def pieces_body(who, mrg_ref, w1_ref, w2_ref, exp_ref, out_ref):
+    def put(rows, value):
+        for d in range(16):
+            out_ref[d, rows, :] = value
+
+    for la in range(8):
+
+        @pl.when(who[1] == la)
+        def _(la=la):
+            if la < 4:
+                put(slice(0, 32), mrg_ref[la * 32 : la * 32 + 32, :])
+                put(slice(32, 96), w1_ref[:, la * 256 : la * 256 + 256])
+            else:
+                r, n = (la % 2) * 32, ((la - 4) // 2) * 256
+                put(slice(0, 32), exp_ref[r : r + 32, n : n + 256])
+                k = (la - 4) * 256
+                put(slice(32, 96), w2_ref[k : k + 256, :].astype(F32).T.astype(BF))
+
+
+def pair_of(who, step):
+    return jnp.bitwise_and(who[0] - STEPS[step], 3)
+
+
+def load_out_weights(who, w_refs, wo_ref):
+    for step, ref in enumerate(w_refs):
         for j in range(4):
-            wo_ref[m * 128 : m * 128 + 128, j * 128 : j * 128 + 128] = w_ref[
-                m, j * 128 : j * 128 + 128, 384:512
+            wo_ref[pair_of(who, step), :, j * 128 : j * 128 + 128] = ref[
+                j * 128 : j * 128 + 128, 384:512
             ]
 
 
-def forward_body(who, scales, x_ref, w_ref, g_ref, hid_ref, mrg_ref, stk_ref, wo_ref, mix_ref):
+def forward_body(
+    who, scales, x_ref, w0, w1, w2, w3, g_ref, hid_ref, mrg_ref, stk_ref, wo_ref, mix_ref
+):
     split = jnp.where(jnp.logical_and(who[1] == who[3] - 1, who[0] >= 2), 1, 0)
-    load_out_weights(w_ref, wo_ref)
+    load_out_weights(who, (w0, w1, w2, w3), wo_ref)
     ones = segments()
     x = x_ref[...].astype(F32)
     (center,), scale = norm_parts([x], 512)
     normed = (center * scale).astype(BF)
-    for p in range(4):
-        stacked = dot(normed, w_ref[p, :, 0:384]).astype(BF)
-        stk_ref[p] = stacked
+    for step, ref in enumerate((w0, w1, w2, w3)):
+        p = pair_of(who, step)
+        stacked = dot(normed, ref[:, 0:384]).astype(BF)
+        stk_ref[step] = stacked
         soft = attend(
             stacked[:, 0:128],
             stacked[:, 128:256],
@@ -128,8 +145,9 @@
         )[-1].astype(BF)
         values = by_head(stacked[:, 256:384])
         both = jnp.concatenate([soft[0:128], soft[128:256]], 1)
-        mix_ref[:, p * 128 : p * 128 + 128] = dot(both, values).astype(BF)
-    hidden = (x + dot(mix_ref[...], wo_ref[...])).astype(BF)
+        mix_ref[p] = dot(both, values).astype(BF)
+    mixed = jnp.concatenate([mix_ref[p] for p in range(4)], 1)
+    hidden = (x + dot(mixed, wo_ref[...].reshape(512, 512))).astype(BF)
     hid_ref[...] = hidden
     parts = [hidden[i * 32 : i * 32 + 32].astype(F32) for i in range(4)]
     centers, scale = norm_parts(parts, 2048)
@@ -147,15 +165,18 @@
             mrg_ref[d, 40:56, j * 512 : j * 512 + 512] = g_ref[row : row + 16] * fits
 
 
-def backward_body(who, scales, x_ref, dh_ref, stk_ref, w_ref, out_ref, wo_ref, acc_ref):
+def backward_body(
+    who, scales, x_ref, dh_ref, stk_ref, w0, w1, w2, w3, out_ref, wo_ref, acc_ref
+):
     split = jnp.where(jnp.logical_and(who[1] == who[3] - 1, who[0] >= 2), 1, 0)
-    load_out_weights(w_ref, wo_ref)
+    load_out_weights(who, (w0, w1, w2, w3), wo_ref)
     ones = segments()
     dh = dh_ref[...]
-    for p in range(4):
-        stacked = stk_ref[p]
+    for step, ref in enumerate((w0, w1, w2, w3)):
+        p = pair_of(who, step)
+        stacked = stk_ref[step]
         q, k, v = stacked[:, 0:128], stacked[:, 128:256], stacked[:, 256:384]
-        d_mix = dot(dh, wo_ref[p * 128 : p * 128 + 128, :], 1, 1).astype(BF)
+        d_mix = dot(dh, wo_ref[p], 1, 1).astype(BF)
         q_sum, k_sum, q_len, k_len, q_two, k_unit, scale, soft = attend(
             q, k, scales[2 * p], scales[2 * p + 1], split, ones
         )
@@ -177,8 +198,8 @@
         d_stack = jnp.concatenate(
             [unit_back(q, d_q, q_sum, q_len), unit_back(k, d_k, k_sum, k_len), d_v], 1
         )
-        part = dot(d_stack, w_ref[p, :, 0:384], 1, 1)
-        if p == 0:
+        part = dot(d_stack, ref[:, 0:384], 1, 1)
+        if step == 0:
             acc_ref[...] = part
         else:
             acc_ref[...] += part
@@ -201,14 +222,14 @@
 
 def placed(who, refs):
     x, core = who[4], who[2]
-    own, other = refs[0:4], refs[4]
     for step in range(4):
-        yield own[step], jnp.bitwise_and(x - STEPS[step], 3), core
-        yield other.at[step], jnp.bitwise_and(x - STEPS[step], 3), 1 - core
-
-
-def merge_body(who, r0, r1, r2, r3, ro, in_ref, mrg_ref, exp_ref, out_ref):
-    for ref, x, c in placed(who, (r0, r1, r2, r3, ro)):
+        yield refs[2 * step], jnp.bitwise_and(x - STEPS[step], 3), core
+        yield refs[2 * step + 1], jnp.bitwise_and(x - STEPS[step], 3), 1 - core
+
+
+def merge_body(who, *refs):
+    in_ref, mrg_ref, exp_ref, out_ref = refs[8:]
+    for ref, x, c in placed(who, refs):
         for z in range(2):
             for la in range(4):
                 mrg_ref[x, z, c, la * 32 : la * 32 + 32, :] = ref[la, z]
@@ -230,10 +251,9 @@
         out_ref[d, :, 256:1280] = d_out
 
 
-def dense_body(
-    who, r0, r1, r2, r3, ro, in_ref, out_ref, crs_ref, dout_ref, w1_ref, w2_ref
-):
-    for ref, x, c in placed(who, (r0, r1, r2, r3, ro)):
+def dense_body(who, *refs):
+    in_ref, out_ref, crs_ref, dout_ref, w1_ref, w2_ref = refs[8:]
+    for ref, x, c in placed(who, refs):
         for z in range(2):
             for j in range(4):
                 w1_ref[x, z, c, :, j * 256 : j * 256 + 256] = ref[j, z]
@@ -383,26 +403,24 @@
     )
 
     wo_rows = jnp.concatenate([wo[:, j * 128 : j * 128 + 128] for j in range(4)], 0)
-    qkvo = to_all(jnp.concatenate([qk[:, 0], qk[:, 1], wv, wo_rows], 1), "mp")
-
-    def piece(shard):
-        n = shard.shape[0] // lats
-        return lax.dynamic_slice_in_dim(shard, lat * n, n, 0)
-
-    second = w_second.T
-    one = jnp.concatenate([w_merge, w_expand[:, 0:256], w_expand[:, 256:512]], 0)
-    two = jnp.concatenate(
-        [w[:, j * 256 : j * 256 + 256] for w in (w_first, second) for j in range(4)], 0
-    )
-    shards = to_all(jnp.concatenate([piece(one), piece(two)], 0), ("lat", "zh"))
+    qkvo = [jnp.concatenate([qk[:, 0], qk[:, 1], wv, wo_rows], 1)]
+    for step in STEPS[1:]:
+        qkvo.append(lax.ppermute(qkvo[0], "mp", [(i, (i + step) % 4) for i in range(4)]))
+
+    shards = call(pieces_body, arr(16, 96, 256), n_scalar=1, n_in=4)(
+        who, w_merge, w_first, w_second, w_expand
+    )
+    shards = swap(shards, ("lat", "zh"))
     shards = shards.reshape(lats, 2, 96, 256)
 
     def gathered(own):
-        parts = [own]
-        for step in STEPS[1:]:
-            parts.append(lax.ppermute(own, "x", [(i, (i + step) % 4) for i in range(4)]))
-        other = lax.ppermute(jnp.stack(parts), "core", [(0, 1), (1, 0)])
-        return (*parts, other)
+        parts = []
+        for step in STEPS:
+            part = own
+            if step:
+                part = lax.ppermute(own, "x", [(i, (i + step) % 4) for i in range(4)])
+            parts += [part, lax.ppermute(part, "core", [(0, 1), (1, 0)])]
+        return parts
 
     one_parts = gathered(shards[:, :, 0:32])
     two_parts = gathered(shards[:, :, 32:96])
@@ -410,16 +428,16 @@
     hidden, merged, stacked = call(
         forward_body,
         [arr(128, 512), arr(4, 56, 2048), arr(4, 128, 384)],
-        [pltpu.VMEM((512, 512), BF), pltpu.VMEM((128, 512), BF)],
+        [pltpu.VMEM((4, 128, 512), BF), pltpu.VMEM((4, 128, 128), BF)],
         n_scalar=2,
-        n_in=3,
-    )(who, scales, x_win, qkvo, g_strip)
+        n_in=6,
+    )(who, scales, x_win, *qkvo, g_strip)
     merged = swap(merged, "mp")
     merge_full, expand_full, columns = call(
         merge_body,
         [arr(4, 2, 2, 128, 256), arr(4, 2, 2, 64, 512), arr(4, 128, 1280)],
         n_scalar=1,
-        n_in=6,
+        n_in=9,
     )(who, *one_parts, merged)
     merge_full = merge_full.reshape(2048, 256)
     expand_full = expand_full.reshape(1024, 512)
@@ -429,7 +447,7 @@
         [arr(4, 160, 1024), arr(128, 1024), arr(128, 1024)],
         [pltpu.VMEM((4, 2, 2, 64, 1024), BF), pltpu.VMEM((4, 2, 2, 64, 1024), BF)],
         n_scalar=1,
-        n_in=6,
+        n_in=9,
     )(who, *two_parts, columns)
     sums = swap(sums, "mp")
     merges = call(
@@ -446,15 +464,16 @@
     grads = call(
         backward_body,
         arr(4, 64, 512),
-        [pltpu.VMEM((512, 512), BF), pltpu.VMEM((128, 512), F32)],
+        [pltpu.VMEM((4, 128, 512), BF), pltpu.VMEM((128, 512), F32)],
         n_scalar=2,
-        n_in=4,
-    )(who, scales, x_win, d_hidden, stacked, qkvo)
-    grads = swap(grads, "mp")
+        n_in=7,
+    )(who, scales, x_win, d_hidden, stacked, *qkvo)
     added = call(expand_body, arr(4, 96, 512), n_scalar=1, n_in=3)(
         who, merges, hidden, expand_full
     )
     added = swap(added, "mp")
+    grads, added = lax.optimization_barrier((grads, added))
+    grads = swap(grads, "mp")
     out_strip = call(output_body, arr(128, 512), n_scalar=1, n_in=1)(who, added)
     half = ((me + 3) % 4) // 2
     grad_strip = jnp.concatenate(

time: 267 us -> 254 us (0.951)
  the two profiles are of different devices: /device:TPU:6 before, /device:TPU:5 now
where the time goes in v1:
time: 254 us; the launch traced here: 252 us
  starting transfers between devices  128 us (50%)
  waiting for transfers between devices  44.4 us (17%)
  blocking collectives  29.7 us (12%)
  local copies, waits for them, and re-layouts  22.9 us (9%)
  Pallas kernels  22.1 us (9%)
  matrix products  2.64 us (1%)
    all_to_all x5, starting transfers between devices, swap(): return lax.all_to_all(value, axis, 0, 0, tiled=True)  32 us
    all_to_all x2, blocking collectives, swap(): return lax.all_to_all(value, axis, 0, 0, tiled=True)  29.7 us
    ppermute x2, starting transfers between devices, rolled_back(): beyond = lax.ppermute(strip, LONMP, across)  25 us
    ppermute x8, starting transfers between devices, gathered(): parts += [part, lax.ppermute(part, 'core', [(0, 1), (1, 0)])]  22.3 us
    ppermute x6, starting transfers between devices, gathered(): part = lax.ppermute(own, 'x', [(i, (i + step) % 4) for i in range(4)])  20.1 us
    unnamed x85, local copies, waits for them, and re-layouts  18 us
    ppermute x1, waiting for transfers between devices, whole_step(): came = lax.ppermute(sent, LON, [(i, (i - 1) % lons) for i in range(lons)])  13.9 us
    ppermute x1, waiting for transfers between devices, whole_step(): rows = lax.ppermute(rows, 'lat', [(i, (i - 1) % lats) for i in range(lats)])  13.8 us
  transfers between devices with their start and end apart: 28, of which 5 were waited for; matrix products, arithmetic and copies ran while one was open for 3% of the time, Pallas kernels for 6%

profile of v1, /device:TPU:5, one launch (start us, length us, event | category | flops | bytes accessed | tf_op | source)
XLA Modules:
  0.0 252.2 jit_solution(4979288508147589614)
XLA Ops:
  5.9 14.9 %all-to-all-start = ((bf16[16,96,256]{2,1,0:T(8,128)(2,1)}), bf16[16,96,256]{2,1,0:T(8,128)(2,1)S(1)}, u32[]{:S(2)}, u32[]{:S(2)}) async-start(bf16[16,96,256]{2,1,0:T(8,128)(2,1)} %shard_map.266), calls=%async_computation | async-start | bytes 1572864 | tf_op jit(solution)/shard_map/all_to_all | solution.py:22
  21.8 3.2 %collective-permute-start.16 = (bf16[512,512]{1,0:T(8,128)(2,1)S(1)}, bf16[512,512]{1,0:T(8,128)(2,1)S(1)}, u32[]{:S(2)}, u32[]{:S(2)}) collective-permute-start(bf16[512,512]{1,0:T(8,128)(2,1)S(1)} %maximum_maximum_fusion.w0), channel_id=1, source_target_pairs={{0,1},{1,2},{2,3},{3,0},{4,5},{5,6},{6,7},{7,4},{8,9},{9,10},{10,1... | collective-permute-start | bytes 1572872 | tf_op jit(solution)/shard_map/ppermute | solution.py:408
  25.1 3.4 %collective-permute-start.17 = (bf16[512,512]{1,0:T(8,128)(2,1)S(1)}, bf16[512,512]{1,0:T(8,128)(2,1)S(1)}, u32[]{:S(2)}, u32[]{:S(2)}) collective-permute-start(bf16[512,512]{1,0:T(8,128)(2,1)S(1)} %maximum_maximum_fusion.w0), channel_id=1, source_target_pairs={{0,3},{1,0},{2,1},{3,2},{4,7},{5,4},{6,5},{7,6},{8,11},{9,8},{10,9... | collective-permute-start | bytes 1572872 | tf_op jit(solution)/shard_map/ppermute | solution.py:408
  28.4 3.5 %collective-permute-start.18 = (bf16[512,512]{1,0:T(8,128)(2,1)S(1)}, bf16[512,512]{1,0:T(8,128)(2,1)S(1)}, u32[]{:S(2)}, u32[]{:S(2)}) collective-permute-start(bf16[512,512]{1,0:T(8,128)(2,1)S(1)} %maximum_maximum_fusion.w0), channel_id=1, source_target_pairs={{0,2},{1,3},{2,0},{3,1},{4,6},{5,7},{6,4},{7,5},{8,10},{9,11},{10,... | collective-permute-start | bytes 1572872 | tf_op jit(solution)/shard_map/ppermute | solution.py:408
  32.9 9.9 %collective-permute-start = (bf16[160,512]{1,0:T(8,128)(2,1)S(1)}, bf16[160,512]{1,0:T(8,128)(2,1)S(1)}, u32[]{:S(2)}, u32[]{:S(2)}) collective-permute-start(bf16[160,512]{1,0:T(8,128)(2,1)S(1)} %pad_maximum_fusion.1), channel_id=1, source_target_pairs={{0,448},{64,0},{128,64},{192,128},{256,192},{320,256},{384,320},{4... | collective-permute-start | bytes 491528 | tf_op jit(solution)/shard_map/ppermute | solution.py:387
  42.9 13.8 %collective-permute-done = bf16[160,512]{1,0:T(8,128)(2,1)S(1)} collective-permute-done((bf16[160,512]{1,0:T(8,128)(2,1)S(1)}, bf16[160,512]{1,0:T(8,128)(2,1)S(1)}, u32[]{:S(2)}, u32[]{:S(2)}) %collective-permute-start) | collective-permute-done | bytes 163872 | tf_op jit(solution)/shard_map/ppermute | solution.py:387
  58.2 4.3 %collective-permute-start.1 = (bf16[128,512]{1,0:T(8,128)(2,1)S(1)}, bf16[128,512]{1,0:T(8,128)(2,1)S(1)}, u32[]{:S(2)}, u32[]{:S(2)}) collective-permute-start(bf16[128,512]{1,0:T(8,128)(2,1)S(1)} %convolution_convert_fusion.2), channel_id=1, source_target_pairs={{0,60},{4,0},{8,4},{12,8},{16,12},{20,16},{24,20},{28,24},{32,28},... | collective-permute-start | bytes 393224 | tf_op jit(solution)/shard_map/ppermute | solution.py:394
  62.5 13.9 %collective-permute-done.1 = bf16[128,512]{1,0:T(8,128)(2,1)S(1)} collective-permute-done((bf16[128,512]{1,0:T(8,128)(2,1)S(1)}, bf16[128,512]{1,0:T(8,128)(2,1)S(1)}, u32[]{:S(2)}, u32[]{:S(2)}) %collective-permute-start.1) | collective-permute-done | bytes 131104 | tf_op jit(solution)/shard_map/ppermute | solution.py:394
  77.5 4.8 %shard_map.267 = (bf16[128,512]{1,0:T(8,128)(2,1)S(1)}, bf16[4,56,2048]{2,1,0:T(8,128)(2,1)}, bf16[4,128,384]{2,1,0:T(8,128)(2,1)S(1)}) custom-call(s32[5]{0:T(128)S(1)} %stack.19.who, f32[8]{0:T(128)S(1)} %copy-done.25, bf16[128,512]{1,0:T(8,128)(2,1)S(1)} %convolution_convert_fusion.1.x_ref, bf16[512,512]{1,0:T(8,128)(2,1)S(1)} %maximum_maximum_fusion.w0, ...), custom_call_target="tpu_custom_call" | custom-call | tf_op jit(solution)/shard_map/pallas_call | solution.py:428
  83.1 4.2 %all-to-all-start.1 = ((bf16[4,56,2048]{2,1,0:T(8,128)(2,1)}), bf16[4,56,2048]{2,1,0:T(8,128)(2,1)S(1)}, u32[]{:S(2)}, u32[]{:S(2)}) async-start(bf16[4,56,2048]{2,1,0:T(8,128)(2,1)} %get-tuple-element.13), calls=%async_computation.1 | async-start | bytes 1835008 | tf_op jit(solution)/shard_map/all_to_all | solution.py:22
  87.3 2.8 %collective-permute-start.10 = (bf16[8,2,32,256]{3,2,1,0:T(8,128)(2,1)S(1)}, bf16[8,2,32,256]{3,2,1,0:T(8,128)(2,1)S(1)}, u32[]{:S(2)}, u32[]{:S(2)}) collective-permute-start(bf16[8,2,32,256]{3,2,1,0:T(8,128)(2,1)S(1)} %slice.76.refs_0_), channel_id=1, source_target_pairs={{0,16},{16,32},{32,48},{48,0},{1,17},{17,33},{33,49},{49,1},{2,18}... | collective-permute-start | bytes 786440 | tf_op jit(solution)/shard_map/ppermute | solution.py:421
  90.1 2.5 collective-permute-start.12
  92.6 3.3 %collective-permute-start.14 = (bf16[8,2,32,256]{3,2,1,0:T(8,128)(2,1)S(1)}, bf16[8,2,32,256]{3,2,1,0:T(8,128)(2,1)S(1)}, u32[]{:S(2)}, u32[]{:S(2)}) collective-permute-start(bf16[8,2,32,256]{3,2,1,0:T(8,128)(2,1)S(1)} %slice.76.refs_0_), channel_id=1, source_target_pairs={{0,32},{16,48},{32,0},{48,16},{1,33},{17,49},{33,1},{49,17},{2,34}... | collective-permute-start | bytes 786440 | tf_op jit(solution)/shard_map/ppermute | solution.py:421
  96.0 6.6 %collective-permute-start.9 = (bf16[8,2,32,256]{3,2,1,0:T(8,128)(2,1)S(1)}, bf16[8,2,32,256]{3,2,1,0:T(8,128)(2,1)S(1)}, u32[]{:S(2)}, u32[]{:S(2)}) collective-permute-start(bf16[8,2,32,256]{3,2,1,0:T(8,128)(2,1)S(1)} %slice.76.refs_0_), channel_id=1, source_target_pairs={{0,4},{4,0},{1,5},{5,1},{2,6},{6,2},{3,7},{7,3},{8,12},{12,8},{9,1... | collective-permute-start | bytes 786440 | tf_op jit(solution)/shard_map/ppermute | solution.py:422
  104.5 2.4 collective-permute-start.13
  106.9 1.9 collective-permute-start.15
  110.7 5.9 %collective-permute-start.3 = (bf16[8,2,64,256]{3,2,1,0:T(8,128)(2,1)}, bf16[8,2,64,256]{3,2,1,0:T(8,128)(2,1)}, u32[]{:S(2)}, u32[]{:S(2)}) collective-permute-start(bf16[8,2,64,256]{3,2,1,0:T(8,128)(2,1)} %slice.75.refs_0_), channel_id=1, source_target_pairs={{0,16},{16,32},{32,48},{48,0},{1,17},{17,33},{33,49},{49,1},{2,18}... | collective-permute-start | bytes 1572872 | tf_op jit(solution)/shard_map/ppermute | solution.py:421
  116.6 1.9 collective-permute-start.5
  119.3 3.7 %collective-permute-start.7 = (bf16[8,2,64,256]{3,2,1,0:T(8,128)(2,1)}, bf16[8,2,64,256]{3,2,1,0:T(8,128)(2,1)}, u32[]{:S(2)}, u32[]{:S(2)}) collective-permute-start(bf16[8,2,64,256]{3,2,1,0:T(8,128)(2,1)} %slice.75.refs_0_), channel_id=1, source_target_pairs={{0,32},{16,48},{32,0},{48,16},{1,33},{17,49},{33,1},{49,17},{2,34}... | collective-permute-start | bytes 1572872 | tf_op jit(solution)/shard_map/ppermute | solution.py:421
  128.7 4.4 %all-to-all-start.2 = ((bf16[4,128,1280]{2,1,0:T(8,128)(2,1)}), bf16[4,128,1280]{2,1,0:T(8,128)(2,1)S(1)}, u32[]{:S(2)}, u32[]{:S(2)}) async-start(bf16[4,128,1280]{2,1,0:T(8,128)(2,1)} %copy-done.5), calls=%async_computation.2 | async-start | bytes 2621440 | tf_op jit(solution)/shard_map/all_to_all | solution.py:22
  133.1 3.2 %collective-permute-start.2 = (bf16[8,2,64,256]{3,2,1,0:T(8,128)(2,1)}, bf16[8,2,64,256]{3,2,1,0:T(8,128)(2,1)S(1)}, u32[]{:S(2)}, u32[]{:S(2)}) collective-permute-start(bf16[8,2,64,256]{3,2,1,0:T(8,128)(2,1)} %slice.75.refs_0_), channel_id=1, source_target_pairs={{0,4},{4,0},{1,5},{5,1},{2,6},{6,2},{3,7},{7,3},{8,12},{12,8},{9,1... | collective-permute-start | bytes 1572872 | tf_op jit(solution)/shard_map/ppermute | solution.py:422
  138.3 2.4 collective-permute-start.6
  145.9 3.8 %all-to-all-done.2.refs_8_ = bf16[4,128,1280]{2,1,0:T(8,128)(2,1)S(1)} async-done(((bf16[4,128,1280]{2,1,0:T(8,128)(2,1)}), bf16[4,128,1280]{2,1,0:T(8,128)(2,1)S(1)}, u32[]{:S(2)}, u32[]{:S(2)}) %all-to-all-start.2) | async-done | bytes 1310752 | tf_op jit(solution)/shard_map/all_to_all | solution.py:22
  153.9 4.2 %shard_map.269 = (bf16[4,160,1024]{2,1,0:T(8,128)(2,1)S(1)}, bf16[128,1024]{1,0:T(8,128)(2,1)S(1)}, bf16[128,1024]{1,0:T(8,128)(2,1)S(1)}) custom-call(s32[5]{0:T(128)S(1)} %stack.19.who, bf16[8,2,64,256]{3,2,1,0:T(8,128)(2,1)} %slice.75.refs_0_, bf16[8,2,64,256]{3,2,1,0:T(8,128)(2,1)S(1)} %copy-done.11, ...), custom_call_target="tpu_custom_call" | custom-call | tf_op jit(solution)/shard_map/pallas_call | solution.py:445
  158.1 18.1 %all_to_all.35.recv_ref = bf16[4,160,1024]{2,1,0:T(8,128)(2,1)S(1)} all-to-all(bf16[4,160,1024]{2,1,0:T(8,128)(2,1)S(1)} %get-tuple-element.15), channel_id=1, replica_groups=mesh['lat'=8,'x'=4,'zh'=2,'core'=2,'mp'=4] {'mp'}, dimensions={0} | all-to-all | bytes 2621440 | tf_op jit(solution)/shard_map/all_to_all | solution.py:22
  177.8 11.6 %all_to_all.36.recv_ref = bf16[4,32,3072]{2,1,0:T(8,128)(2,1)S(1)} all-to-all(bf16[4,32,3072]{2,1,0:T(8,128)(2,1)S(1)} %shard_map.270), channel_id=1, replica_groups=mesh['lat'=8,'x'=4,'zh'=2,'core'=2,'mp'=4] {'mp'}, dimensions={0} | all-to-all | bytes 1572864 | tf_op jit(solution)/shard_map/all_to_all | solution.py:22
  191.0 4.4 %all-to-all-start.5 = ((bf16[4,96,512]{2,1,0:T(8,128)(2,1)}), bf16[4,96,512]{2,1,0:T(8,128)(2,1)}, u32[]{:S(2)}, u32[]{:S(2)}) async-start(bf16[4,96,512]{2,1,0:T(8,128)(2,1)} %copy-done.4), calls=%async_computation.5 | async-start | bytes 786432 | tf_op jit(solution)/shard_map/all_to_all | solution.py:22
  197.7 5.5 %shard_map.272 = bf16[4,64,512]{2,1,0:T(8,128)(2,1)} custom-call(s32[5]{0:T(128)S(1)} %stack.19.who, f32[8]{0:T(128)S(1)} %copy-done.25, bf16[128,512]{1,0:T(8,128)(2,1)S(1)} %convolution_convert_fusion.1.x_ref, bf16[128,512]{1,0:T(8,128)(2,1)S(1)} %shard_map.271.dh_ref, bf16[4,128,384]{2,1,0:T(8,128)(2,1)S(1)} %copy-done.19, ...), custom_call_target="tpu_custom_call" | custom-call | tf_op jit(solution)/shard_map/pallas_call | solution.py:464
  203.2 4.1 %all-to-all-start.6 = ((bf16[4,64,512]{2,1,0:T(8,128)(2,1)}), bf16[4,64,512]{2,1,0:T(8,128)(2,1)S(1)}, u32[]{:S(2)}, u32[]{:S(2)}) async-start(bf16[4,64,512]{2,1,0:T(8,128)(2,1)} %shard_map.272), calls=%async_computation.6 | async-start | bytes 524288 | tf_op jit(solution)/shard_map/all_to_all | solution.py:22
  208.3 14.6 %collective-permute-start.19 = (bf16[128,512]{1,0:T(8,128)(2,1)S(1)}, bf16[128,512]{1,0:T(8,128)(2,1)S(1)}, u32[]{:S(2)}, u32[]{:S(2)}) collective-permute-start(bf16[128,512]{1,0:T(8,128)(2,1)S(1)} %shard_map.274), channel_id=1, source_target_pairs={{0,4},{4,8},{8,12},{12,16},{16,20},{20,24},{24,28},{28,32},{32,36}... | collective-permute-start | bytes 393224 | tf_op jit(solution)/shard_map/ppermute | solution.py:502
  225.0 10.5 %collective-permute-start.21 = (bf16[128,512]{1,0:T(8,128)(2,1)S(1)}, bf16[128,512]{1,0:T(8,128)(2,1)S(1)}, u32[]{:S(2)}, u32[]{:S(2)}) collective-permute-start(bf16[128,512]{1,0:T(8,128)(2,1)S(1)} %pad_maximum_fusion.4), channel_id=1, source_target_pairs={{0,4},{4,8},{8,12},{12,16},{16,20},{20,24},{24,28},{28,32},{32,36}... | collective-permute-start | bytes 393224 | tf_op jit(solution)/shard_map/ppermute | solution.py:502
  238.7 12.5 %collective-permute-done.22 = bf16[32,512]{1,0:T(8,128)(2,1)S(1)} collective-permute-done((bf16[32,512]{1,0:T(8,128)(2,1)S(1)}, bf16[32,512]{1,0:T(8,128)(2,1)S(1)}, u32[]{:S(2)}, u32[]{:S(2)}) %collective-permute-start.22) | collective-permute-done | bytes 32800 | tf_op jit(solution)/shard_map/ppermute | solution.py:504
  (150 shorter events, 44.4 us)
Async XLA Ops:
  5.9 77.1 %all-to-all-start = ((bf16[16,96,256]{2,1,0:T(8,128)(2,1)}), bf16[16,96,256]{2,1,0:T(8,128)(2,1)S(1)}, u32[]{:S(2)}, u32[]{:S(2)}) async-start(bf16[16,96,256]{2,1,0:T(8,128)(2,1)} %shard_map.266), calls=%async_computation | async-start | bytes 1572864 | tf_op jit(solution)/shard_map/all_to_all | solution.py:22
  21.3 21.5 %copy-start.40 = (s32[128]{0:T(128)S(1)}, s32[128]{0:T(128)}, u32[]{:S(2)}) copy-start(s32[128]{0:T(128)} %constant.119.clone) | copy-start | bytes 1540
  21.3 21.5 %copy-start.41 = (s32[128]{0:T(128)S(1)}, s32[128]{0:T(128)}, u32[]{:S(2)}) copy-start(s32[128]{0:T(128)} %constant.120.clone) | copy-start | bytes 1540
  21.8 55.3 %collective-permute-start.16 = (bf16[512,512]{1,0:T(8,128)(2,1)S(1)}, bf16[512,512]{1,0:T(8,128)(2,1)S(1)}, u32[]{:S(2)}, u32[]{:S(2)}) collective-permute-start(bf16[512,512]{1,0:T(8,128)(2,1)S(1)} %maximum_maximum_fusion.w0), channel_id=1, source_target_pairs={{0,1},{1,2},{2,3},{3,0},{4,5},{5,6},{6,7},{7,4},{8,9},{9,10},{10,1... | collective-permute-start | bytes 1572872 | tf_op jit(solution)/shard_map/ppermute | solution.py:408
  25.1 52.1 %collective-permute-start.17 = (bf16[512,512]{1,0:T(8,128)(2,1)S(1)}, bf16[512,512]{1,0:T(8,128)(2,1)S(1)}, u32[]{:S(2)}, u32[]{:S(2)}) collective-permute-start(bf16[512,512]{1,0:T(8,128)(2,1)S(1)} %maximum_maximum_fusion.w0), channel_id=1, source_target_pairs={{0,3},{1,0},{2,1},{3,2},{4,7},{5,4},{6,5},{7,6},{8,11},{9,8},{10,9... | collective-permute-start | bytes 1572872 | tf_op jit(solution)/shard_map/ppermute | solution.py:408
  28.4 48.8 %collective-permute-start.18 = (bf16[512,512]{1,0:T(8,128)(2,1)S(1)}, bf16[512,512]{1,0:T(8,128)(2,1)S(1)}, u32[]{:S(2)}, u32[]{:S(2)}) collective-permute-start(bf16[512,512]{1,0:T(8,128)(2,1)S(1)} %maximum_maximum_fusion.w0), channel_id=1, source_target_pairs={{0,2},{1,3},{2,0},{3,1},{4,6},{5,7},{6,4},{7,5},{8,10},{9,11},{10,... | collective-permute-start | bytes 1572872 | tf_op jit(solution)/shard_map/ppermute | solution.py:408
  32.9 23.7 %collective-permute-start = (bf16[160,512]{1,0:T(8,128)(2,1)S(1)}, bf16[160,512]{1,0:T(8,128)(2,1)S(1)}, u32[]{:S(2)}, u32[]{:S(2)}) collective-permute-start(bf16[160,512]{1,0:T(8,128)(2,1)S(1)} %pad_maximum_fusion.1), channel_id=1, source_target_pairs={{0,448},{64,0},{128,64},{192,128},{256,192},{320,256},{384,320},{4... | collective-permute-start | bytes 491528 | tf_op jit(solution)/shard_map/ppermute | solution.py:387
  56.7 19.8 %copy-start.31 = (bf16[2,16,16,512]{3,2,1,0:T(8,128)(2,1)S(1)}, bf16[2,16,16,512]{3,2,1,0:T(8,128)(2,1)}, u32[]{:S(2)}) copy-start(bf16[2,16,16,512]{3,2,1,0:T(8,128)(2,1)} %param.27) | copy-start | bytes 1572868
  58.2 18.3 %collective-permute-start.1 = (bf16[128,512]{1,0:T(8,128)(2,1)S(1)}, bf16[128,512]{1,0:T(8,128)(2,1)S(1)}, u32[]{:S(2)}, u32[]{:S(2)}) collective-permute-start(bf16[128,512]{1,0:T(8,128)(2,1)S(1)} %convolution_convert_fusion.2), channel_id=1, source_target_pairs={{0,60},{4,0},{8,4},{12,8},{16,12},{20,16},{24,20},{28,24},{32,28},... | collective-permute-start | bytes 393224 | tf_op jit(solution)/shard_map/ppermute | solution.py:394
  83.1 39.9 %all-to-all-start.1 = ((bf16[4,56,2048]{2,1,0:T(8,128)(2,1)}), bf16[4,56,2048]{2,1,0:T(8,128)(2,1)S(1)}, u32[]{:S(2)}, u32[]{:S(2)}) async-start(bf16[4,56,2048]{2,1,0:T(8,128)(2,1)} %get-tuple-element.13), calls=%async_computation.1 | async-start | bytes 1835008 | tf_op jit(solution)/shard_map/all_to_all | solution.py:22
  87.3 15.2 %collective-permute-start.10 = (bf16[8,2,32,256]{3,2,1,0:T(8,128)(2,1)S(1)}, bf16[8,2,32,256]{3,2,1,0:T(8,128)(2,1)S(1)}, u32[]{:S(2)}, u32[]{:S(2)}) collective-permute-start(bf16[8,2,32,256]{3,2,1,0:T(8,128)(2,1)S(1)} %slice.76.refs_0_), channel_id=1, source_target_pairs={{0,16},{16,32},{32,48},{48,0},{1,17},{17,33},{33,49},{49,1},{2,18}... | collective-permute-start | bytes 786440 | tf_op jit(solution)/shard_map/ppermute | solution.py:421
  90.1 14.3 %collective-permute-start.12 = (bf16[8,2,32,256]{3,2,1,0:T(8,128)(2,1)S(1)}, bf16[8,2,32,256]{3,2,1,0:T(8,128)(2,1)S(1)}, u32[]{:S(2)}, u32[]{:S(2)}) collective-permute-start(bf16[8,2,32,256]{3,2,1,0:T(8,128)(2,1)S(1)} %slice.76.refs_0_), channel_id=1, source_target_pairs={{0,48},{16,0},{32,16},{48,32},{1,49},{17,1},{33,17},{49,33},{2,50}... | collective-permute-start | bytes 786440 | tf_op jit(solution)/shard_map/ppermute | solution.py:421
  92.6 14.3 %collective-permute-start.14 = (bf16[8,2,32,256]{3,2,1,0:T(8,128)(2,1)S(1)}, bf16[8,2,32,256]{3,2,1,0:T(8,128)(2,1)S(1)}, u32[]{:S(2)}, u32[]{:S(2)}) collective-permute-start(bf16[8,2,32,256]{3,2,1,0:T(8,128)(2,1)S(1)} %slice.76.refs_0_), channel_id=1, source_target_pairs={{0,32},{16,48},{32,0},{48,16},{1,33},{17,49},{33,1},{49,17},{2,34}... | collective-permute-start | bytes 786440 | tf_op jit(solution)/shard_map/ppermute | solution.py:421
  96.0 20.7 %collective-permute-start.9 = (bf16[8,2,32,256]{3,2,1,0:T(8,128)(2,1)S(1)}, bf16[8,2,32,256]{3,2,1,0:T(8,128)(2,1)S(1)}, u32[]{:S(2)}, u32[]{:S(2)}) collective-permute-start(bf16[8,2,32,256]{3,2,1,0:T(8,128)(2,1)S(1)} %slice.76.refs_0_), channel_id=1, source_target_pairs={{0,4},{4,0},{1,5},{5,1},{2,6},{6,2},{3,7},{7,3},{8,12},{12,8},{9,1... | collective-permute-start | bytes 786440 | tf_op jit(solution)/shard_map/ppermute | solution.py:422
  102.5 16.0 %collective-permute-start.11 = (bf16[8,2,32,256]{3,2,1,0:T(8,128)(2,1)S(1)}, bf16[8,2,32,256]{3,2,1,0:T(8,128)(2,1)S(1)}, u32[]{:S(2)}, u32[]{:S(2)}) collective-permute-start(bf16[8,2,32,256]{3,2,1,0:T(8,128)(2,1)S(1)} %collective-permute-done.10.refs_2_), channel_id=1, source_target_pairs={{0,4},{4,0},{1,5},{5,1},{2,6},{6,2},{3,7},{7,3},{8,12},{12,8},{9,1... | collective-permute-start | bytes 786440 | tf_op jit(solution)/shard_map/ppermute | solution.py:422
  104.5 18.5 %collective-permute-start.13 = (bf16[8,2,32,256]{3,2,1,0:T(8,128)(2,1)S(1)}, bf16[8,2,32,256]{3,2,1,0:T(8,128)(2,1)}, u32[]{:S(2)}, u32[]{:S(2)}) collective-permute-start(bf16[8,2,32,256]{3,2,1,0:T(8,128)(2,1)S(1)} %collective-permute-done.12.refs_4_), channel_id=1, source_target_pairs={{0,4},{4,0},{1,5},{5,1},{2,6},{6,2},{3,7},{7,3},{8,12},{12,8},{9,1... | collective-permute-start | bytes 786440 | tf_op jit(solution)/shard_map/ppermute | solution.py:422
  106.9 16.1 %collective-permute-start.15 = (bf16[8,2,32,256]{3,2,1,0:T(8,128)(2,1)S(1)}, bf16[8,2,32,256]{3,2,1,0:T(8,128)(2,1)}, u32[]{:S(2)}, u32[]{:S(2)}) collective-permute-start(bf16[8,2,32,256]{3,2,1,0:T(8,128)(2,1)S(1)} %collective-permute-done.14.refs_6_), channel_id=1, source_target_pairs={{0,4},{4,0},{1,5},{5,1},{2,6},{6,2},{3,7},{7,3},{8,12},{12,8},{9,1... | collective-permute-start | bytes 786440 | tf_op jit(solution)/shard_map/ppermute | solution.py:422
  110.7 25.6 %collective-permute-start.3 = (bf16[8,2,64,256]{3,2,1,0:T(8,128)(2,1)}, bf16[8,2,64,256]{3,2,1,0:T(8,128)(2,1)}, u32[]{:S(2)}, u32[]{:S(2)}) collective-permute-start(bf16[8,2,64,256]{3,2,1,0:T(8,128)(2,1)} %slice.75.refs_0_), channel_id=1, source_target_pairs={{0,16},{16,32},{32,48},{48,0},{1,17},{17,33},{33,49},{49,1},{2,18}... | collective-permute-start | bytes 1572872 | tf_op jit(solution)/shard_map/ppermute | solution.py:421
  116.6 21.6 %collective-permute-start.5 = (bf16[8,2,64,256]{3,2,1,0:T(8,128)(2,1)}, bf16[8,2,64,256]{3,2,1,0:T(8,128)(2,1)}, u32[]{:S(2)}, u32[]{:S(2)}) collective-permute-start(bf16[8,2,64,256]{3,2,1,0:T(8,128)(2,1)} %slice.75.refs_0_), channel_id=1, source_target_pairs={{0,48},{16,0},{32,16},{48,32},{1,49},{17,1},{33,17},{49,33},{2,50}... | collective-permute-start | bytes 1572872 | tf_op jit(solution)/shard_map/ppermute | solution.py:421
  119.3 21.4 %collective-permute-start.7 = (bf16[8,2,64,256]{3,2,1,0:T(8,128)(2,1)}, bf16[8,2,64,256]{3,2,1,0:T(8,128)(2,1)}, u32[]{:S(2)}, u32[]{:S(2)}) collective-permute-start(bf16[8,2,64,256]{3,2,1,0:T(8,128)(2,1)} %slice.75.refs_0_), channel_id=1, source_target_pairs={{0,32},{16,48},{32,0},{48,16},{1,33},{17,49},{33,1},{49,17},{2,34}... | collective-permute-start | bytes 1572872 | tf_op jit(solution)/shard_map/ppermute | solution.py:421
  128.7 21.0 %all-to-all-start.2 = ((bf16[4,128,1280]{2,1,0:T(8,128)(2,1)}), bf16[4,128,1280]{2,1,0:T(8,128)(2,1)S(1)}, u32[]{:S(2)}, u32[]{:S(2)}) async-start(bf16[4,128,1280]{2,1,0:T(8,128)(2,1)} %copy-done.5), calls=%async_computation.2 | async-start | bytes 2621440 | tf_op jit(solution)/shard_map/all_to_all | solution.py:22
  133.1 9.5 %collective-permute-start.2 = (bf16[8,2,64,256]{3,2,1,0:T(8,128)(2,1)}, bf16[8,2,64,256]{3,2,1,0:T(8,128)(2,1)S(1)}, u32[]{:S(2)}, u32[]{:S(2)}) collective-permute-start(bf16[8,2,64,256]{3,2,1,0:T(8,128)(2,1)} %slice.75.refs_0_), channel_id=1, source_target_pairs={{0,4},{4,0},{1,5},{5,1},{2,6},{6,2},{3,7},{7,3},{8,12},{12,8},{9,1... | collective-permute-start | bytes 1572872 | tf_op jit(solution)/shard_map/ppermute | solution.py:422
  136.3 7.1 %collective-permute-start.4 = (bf16[8,2,64,256]{3,2,1,0:T(8,128)(2,1)}, bf16[8,2,64,256]{3,2,1,0:T(8,128)(2,1)S(1)}, u32[]{:S(2)}, u32[]{:S(2)}) collective-permute-start(bf16[8,2,64,256]{3,2,1,0:T(8,128)(2,1)} %collective-permute-done.3.refs_2_), channel_id=1, source_target_pairs={{0,4},{4,0},{1,5},{5,1},{2,6},{6,2},{3,7},{7,3},{8,12},{12,8},{9,1... | collective-permute-start | bytes 1572872 | tf_op jit(solution)/shard_map/ppermute | solution.py:422
  138.3 6.0 %collective-permute-start.6 = (bf16[8,2,64,256]{3,2,1,0:T(8,128)(2,1)}, bf16[8,2,64,256]{3,2,1,0:T(8,128)(2,1)S(1)}, u32[]{:S(2)}, u32[]{:S(2)}) collective-permute-start(bf16[8,2,64,256]{3,2,1,0:T(8,128)(2,1)} %collective-permute-done.5.refs_4_), channel_id=1, source_target_pairs={{0,4},{4,0},{1,5},{5,1},{2,6},{6,2},{3,7},{7,3},{8,12},{12,8},{9,1... | collective-permute-start | bytes 1572872 | tf_op jit(solution)/shard_map/ppermute | solution.py:422
  140.7 4.5 %collective-permute-start.8 = (bf16[8,2,64,256]{3,2,1,0:T(8,128)(2,1)}, bf16[8,2,64,256]{3,2,1,0:T(8,128)(2,1)S(1)}, u32[]{:S(2)}, u32[]{:S(2)}) collective-permute-start(bf16[8,2,64,256]{3,2,1,0:T(8,128)(2,1)} %collective-permute-done.7.refs_6_), channel_id=1, source_target_pairs={{0,4},{4,0},{1,5},{5,1},{2,6},{6,2},{3,7},{7,3},{8,12},{12,8},{9,1... | collective-permute-start | bytes 1572872 | tf_op jit(solution)/shard_map/ppermute | solution.py:422
  191.0 12.2 %all-to-all-start.5 = ((bf16[4,96,512]{2,1,0:T(8,128)(2,1)}), bf16[4,96,512]{2,1,0:T(8,128)(2,1)}, u32[]{:S(2)}, u32[]{:S(2)}) async-start(bf16[4,96,512]{2,1,0:T(8,128)(2,1)} %copy-done.4), calls=%async_computation.5 | async-start | bytes 786432 | tf_op jit(solution)/shard_map/all_to_all | solution.py:22
  203.2 34.5 %copy-start.39 = (s32[128]{0:T(128)S(1)}, s32[128]{0:T(128)}, u32[]{:S(2)}) copy-start(s32[128]{0:T(128)} %add_select_fusion) | copy-start | bytes 1540
  203.2 21.7 %all-to-all-start.6 = ((bf16[4,64,512]{2,1,0:T(8,128)(2,1)}), bf16[4,64,512]{2,1,0:T(8,128)(2,1)S(1)}, u32[]{:S(2)}, u32[]{:S(2)}) async-start(bf16[4,64,512]{2,1,0:T(8,128)(2,1)} %shard_map.272), calls=%async_computation.6 | async-start | bytes 524288 | tf_op jit(solution)/shard_map/all_to_all | solution.py:22
  208.3 29.4 %collective-permute-start.19 = (bf16[128,512]{1,0:T(8,128)(2,1)S(1)}, bf16[128,512]{1,0:T(8,128)(2,1)S(1)}, u32[]{:S(2)}, u32[]{:S(2)}) collective-permute-start(bf16[128,512]{1,0:T(8,128)(2,1)S(1)} %shard_map.274), channel_id=1, source_target_pairs={{0,4},{4,8},{8,12},{12,16},{16,20},{20,24},{24,28},{28,32},{32,36}... | collective-permute-start | bytes 393224 | tf_op jit(solution)/shard_map/ppermute | solution.py:502
  223.0 14.7 %collective-permute-start.20 = (bf16[32,512]{1,0:T(8,128)(2,1)S(1)}, bf16[32,512]{1,0:T(8,128)(2,1)S(1)}, u32[]{:S(2)}, u32[]{:S(2)}) collective-permute-start(bf16[32,512]{1,0:T(8,128)(2,1)S(1)} %reshape.49), channel_id=1, source_target_pairs={{0,68},{1,65},{2,66},{3,67},{4,72},{5,69},{6,70},{7,71},{8,76},{9,... | collective-permute-start | bytes 98312 | tf_op jit(solution)/shard_map/ppermute | solution.py:504
  225.0 26.3 %collective-permute-start.21 = (bf16[128,512]{1,0:T(8,128)(2,1)S(1)}, bf16[128,512]{1,0:T(8,128)(2,1)S(1)}, u32[]{:S(2)}, u32[]{:S(2)}) collective-permute-start(bf16[128,512]{1,0:T(8,128)(2,1)S(1)} %pad_maximum_fusion.4), channel_id=1, source_target_pairs={{0,4},{4,8},{8,12},{12,16},{16,20},{20,24},{24,28},{28,32},{32,36}... | collective-permute-start | bytes 393224 | tf_op jit(solution)/shard_map/ppermute | solution.py:502
  235.5 15.8 %collective-permute-start.22 = (bf16[32,512]{1,0:T(8,128)(2,1)S(1)}, bf16[32,512]{1,0:T(8,128)(2,1)S(1)}, u32[]{:S(2)}, u32[]{:S(2)}) collective-permute-start(bf16[32,512]{1,0:T(8,128)(2,1)S(1)} %reshape.52), channel_id=1, source_target_pairs={{0,68},{1,65},{2,66},{3,67},{4,72},{5,69},{6,70},{7,71},{8,76},{9,... | collective-permute-start | bytes 98312 | tf_op jit(solution)/shard_map/ppermute | solution.py:504
  (38 other events, 159.5 us)
